TPU v7x, 32 devices: a whole 2x2x4 slice. The times are simulated.
32 devices in a mesh: tile: 8 (over z, x), seg: 4 (over y, core).
Axes of the slice: x: 2, y: 2, z: 4, core: 2. Of those that a mesh axis runs over, the one named last changes fastest.
Arguments:
- shell_state: float32 [4, 128, 64, 1024], P(None, 'tile', 'seg'), may hold values from -6 to 6
- diffusivity: float32 [128, 64, 1024], P('tile', 'seg'), may hold values from 0.02 to 0.16
- inlet_enthalpy: float32 [2048], P('tile'), may hold values from -6 to 6
- transfer_units: float32 [64, 2048], P('seg', 'tile'), as said below
- wall_cells: int32 [32, 32, 512], P(('tile', 'seg')), may hold values from 0 to 262143, as said below
- tube_slots: int32 [64, 2048], P('seg', 'tile'), may hold values from 0 to 16383, as said below
Outputs:
- shell_next: float32 [4, 128, 64, 1024], P(None, 'tile', 'seg')
- enthalpy: float32 [64, 2048], P('seg', 'tile')
Inputs may be any that keep to these rules, and one draw needn't show every extreme that they name: `wall_cells`: entries are local cell numbers of the owner's block. Entry [o, d, j] is the wall cell of the tube cell of device d whose tube_slots entry is o * 512 + j; slots that no tube cell names hold arbitrary cells. `tube_slots`: each entry is o * 512 + j with o an owner device and j < 512; the entries of one device's block are distinct, so one owner serves at most 512 tube cells of one device. `transfer_units`: Positive.
All inputs are finite; a program needn't handle non-finite values.
Results may differ from a plain program's by a relative error of at most 0.00002.
Values sent between devices are 32-bit elements; how exact they have to be, the bound alone decides.
A program may use at most 128 MiB of HBM per device.

v0:
```python
import jax
import jax.numpy as jnp
from jax import lax
from jax.sharding import PartitionSpec as P

DEPOSIT_SCALE = 2.0
LANE_WIDTH = 128
BLOCK_ROWS = 2048


def padded_2(cells, sides, width):
    for axis, dim in sides:
        count = lax.axis_size(axis)
        ends = count - 1
        head = lax.slice_in_dim(cells, 0, width, axis=dim)
        tail = lax.slice_in_dim(cells, cells.shape[dim] - width, cells.shape[dim], axis=dim)
        cells = jnp.concatenate(
            [
                lax.ppermute(tail, axis, [(i, (i + 1) % count) for i in range(ends)]),
                cells,
                lax.ppermute(head, axis, [((i + 1) % count, i) for i in range(ends)]),
            ],
            axis=dim,
        )
    return cells


def prefix(value, axis, join, neutral):
    count, mine = (lax.axis_size(axis), lax.axis_index(axis))
    pieces = jax.tree.map(lambda part: lax.all_gather(part, axis), value)
    total = jax.tree.map(
        lambda part, zero: jnp.full_like(part, 0) + jnp.asarray(zero, part.dtype), value, neutral
    )

    def lap(position, total):
        longer = join(total, jax.tree.map(lambda part: part[position], pieces))
        return jax.tree.map(lambda new, old: jnp.where(position < mine, new, old), longer, total)

    return lax.fori_loop(0, count - 1, lap, total)


def diffuse(state, diffusivity):
    padded = padded_2(state, (("tile", 1), ("seg", 2)), 1)
    neighbours = padded[:, 2:, 1:-1] + padded[:, :-2, 1:-1]
    neighbours = neighbours + padded[:, 1:-1, 2:] + padded[:, 1:-1, :-2]
    z_padded = jnp.pad(state, ((0, 0), (0, 0), (0, 0), (1, 1)))
    neighbours = neighbours + z_padded[..., 2:] + z_padded[..., :-2]
    return state + diffusivity[None] * (neighbours - 6.0 * state)


def compose(earlier, latter):
    return (earlier[0] * latter[0], latter[0] * earlier[1] + latter[1])


def as_lane_rows(flat_table):
    parts = flat_table.shape[0]
    lines = flat_table.shape[1] // LANE_WIDTH
    return jnp.transpose(flat_table.reshape(parts, lines, LANE_WIDTH), (1, 0, 2))


def pick_block(lane_rows, index):
    lanes = lax.broadcasted_iota(jnp.int32, (1, LANE_WIDTH), 1)
    fetched = jnp.take(lane_rows, index // LANE_WIDTH, axis=0)
    chosen = (index % LANE_WIDTH)[:, None] == lanes
    return jnp.sum(jnp.where(chosen[:, None, :], fetched, 0.0), axis=2)


def pick_cells(lane_rows, index):
    count = index.shape[0]
    blocked = index.reshape(count // BLOCK_ROWS, BLOCK_ROWS)
    picked = lax.map(lambda part_index: pick_block(lane_rows, part_index), blocked)
    picked = picked.reshape(count, lane_rows.shape[1])
    return jnp.transpose(picked, (1, 0))


def place_cells(values, index, total):
    lanes = lax.broadcasted_iota(jnp.int32, (1, LANE_WIDTH), 1)
    chosen = (index % LANE_WIDTH)[:, None] == lanes
    spread = jnp.where(chosen, values[:, None], 0.0)
    lines = jnp.zeros((total // LANE_WIDTH, LANE_WIDTH), jnp.float32)
    return lines.at[index // LANE_WIDTH].add(spread).reshape(total)


def body(shell_state, diffusivity, inlet_enthalpy, transfer_units, wall_cells, tube_slots):
    fresh = diffuse(shell_state, diffusivity)
    cell_count = fresh.shape[1] * fresh.shape[2] * fresh.shape[3]
    flat_state = fresh.reshape(4, cell_count)
    push_lists = wall_cells[0]
    devices = push_lists.shape[0]
    capacity = push_lists.shape[1]
    push_flat = push_lists.reshape(-1)
    outgoing = pick_cells(as_lane_rows(flat_state), push_flat).reshape(4, devices, capacity)
    incoming = lax.all_to_all(outgoing, ("tile", "seg"), split_axis=1, concat_axis=1, tiled=True)
    wall_table = incoming.reshape(4, devices * capacity)
    axial_rows = tube_slots.shape[0]
    tube_count = tube_slots.shape[1]
    slot_index = tube_slots.reshape(-1)
    wall_rows = pick_cells(as_lane_rows(wall_table), slot_index).reshape(4, axial_rows, tube_count)
    speed_sq = (
        wall_rows[1] * wall_rows[1] + wall_rows[2] * wall_rows[2] + wall_rows[3] * wall_rows[3]
    )
    decay_rate = jnp.exp(-transfer_units * (1.0 + speed_sq) ** 0.3)
    source = (1.0 - decay_rate) * wall_rows[0]
    step_gain, step_shift = lax.associative_scan(compose, (decay_rate, source), axis=0)
    ones_row = jnp.ones((tube_count,), jnp.float32)
    zeros_row = jnp.zeros((tube_count,), jnp.float32)
    carry_gain, carry_shift = prefix(
        (step_gain[-1], step_shift[-1]), "seg", compose, (ones_row, zeros_row)
    )
    start_enthalpy = carry_gain * inlet_enthalpy + carry_shift
    enthalpy = step_gain * start_enthalpy[None] + step_shift
    prev_enthalpy = jnp.concatenate([start_enthalpy[None], enthalpy[:-1]], axis=0)
    heat_flow = enthalpy - prev_enthalpy
    outbound = place_cells(heat_flow.reshape(-1), slot_index, devices * capacity).reshape(
        devices, capacity
    )
    returned = lax.all_to_all(outbound, ("tile", "seg"), split_axis=0, concat_axis=0, tiled=True)
    deposit = place_cells(returned.reshape(-1), push_flat, cell_count)
    heated = flat_state[0] - DEPOSIT_SCALE * deposit
    shell_next = jnp.concatenate([heated[None], flat_state[1:]], axis=0).reshape(fresh.shape)
    return (shell_next, enthalpy)


def solution(mesh):
    in_specs = (
        P(None, "tile", "seg", None),
        P("tile", "seg", None),
        P("tile"),
        P("seg", "tile"),
        P(("tile", "seg"), None, None),
        P("seg", "tile"),
    )
    out_specs = (P(None, "tile", "seg", None), P("seg", "tile"))
    return jax.shard_map(body, mesh=mesh, in_specs=in_specs, out_specs=out_specs, check_vma=False)
```

profile of v0, /device:TPU:0, one launch (start us, length us, event | category | flops | bytes accessed | tf_op | source)
XLA Modules:
  0.0 722.6 jit_solution(2021986226423027894)
XLA Ops:
  8.8 8.9 %collective-permute-done.1 = f32[4,1,16,1024]{3,2,1,0:T(8,128)S(1)} collective-permute-done((f32[4,1,16,1024]{3,2,1,0:T(8,128)S(1)}, f32[4,1,16,1024]{3,2,1,0:T(8,128)S(1)}, u32[]{:S(2)}, u32[]{:S(2)}) %collective-permute-start.1) | collective-permute-done | bytes 262176 | tf_op jit(solution)/shard_map/ppermute | solution.py:19
  29.3 14.4 %fusion.10 = f32[4,16,16,1024]{3,2,1,0:T(8,128)} fusion(f32[4,16,16,1024]{3,2,1,0:T(8,128)} %param.12, f32[4,18,16,1024]{3,2,1,0:T(8,128)} %copy-done, f32[4,18,1,1024]{3,2,1,0:T(1,128)S(1)} %copy.30, f32[4,18,1,1024]{3,2,1,0:T(1,128)S(1)} %copy.28, f32[4,1,16,1024]{3,2,1,0:T(8,128)S(1)} %collective-permute-done.1, ...), kind=kLoop, calls=%fused_computation.59 | loop fusion | flops 13631488 | bytes 15269888 | tf_op jit(solution)/shard_map/add | solution.py:48
  48.6 7.3 %copy.31 = f32[2048,4,128]{2,1,0:T(4,128)} copy(f32[2048,4,128]{2,0,1:T(8,128)} %bitcast.90) | data formatting | bytes 8388608 | tf_op jit(solution)/shard_map/while | solution.py:71
  55.9 392.0 %while.40 = (s32[]{:T(128)}, f32[8,2048,4]{2,1,0:T(8,128)}, s32[8,2048]{1,0:T(8,128)S(1)}, f32[2048,4,128]{2,1,0:T(4,128)}, s32[]{:T(128)}) while((s32[]{:T(128)}, f32[8,2048,4]{2,1,0:T(8,128)}, s32[8,2048]{1,0:T(8,128)S(1)}, f32[2048,4,128]{2,1,0:T(4,128)}, s32[]{:T(128)}) %tuple.112), condition=%wide.region_2.3_spmd, body=%wide.region_0.2_spmd.sunk | while | flops 3504130 | bytes 14307905 | solution.py:71
  56.0 17.5 %gather_fusion = f32[2048,4,128]{2,1,0:T(4,128)} fusion(f32[2048,4,128]{2,1,0:T(4,128)} %get-tuple-element.449, s32[2048]{0:T(1024)S(1)} %broadcast_clamp_fusion.4), kind=kCustom, calls=%fused_computation.clone.1 | custom fusion | bytes 8396800 | tf_op jit(solution)/shard_map/while/body/eval_jaxpr/jit(_take)/gather | solution.py:63
  73.8 30.0 %select_reduce_fusion.4 = f32[2048,4]{1,0:T(8,128)S(1)} fusion(f32[2048,4,128]{2,1,0:T(4,128)} %gather_fusion, pred[2048]{0:T(1024)(128)(4,1)S(1)} %compare_and_fusion.4, pred[2048,128]{1,0:T(8,128)(4,1)S(1)} %iota_compare_fusion.8), kind=kLoop, calls=%fused_computation.4.clone.1 | loop fusion | flops 3137536 | bytes 4491264 | tf_op jit(solution)/shard_map/while/body/eval_jaxpr/reduce_sum | solution.py:65
  104.9 17.5 %gather_fusion = f32[2048,4,128]{2,1,0:T(4,128)} fusion(f32[2048,4,128]{2,1,0:T(4,128)} %get-tuple-element.449, s32[2048]{0:T(1024)S(1)} %broadcast_clamp_fusion.4), kind=kCustom, calls=%fused_computation.clone.1 | custom fusion | bytes 8396800 | tf_op jit(solution)/shard_map/while/body/eval_jaxpr/jit(_take)/gather | solution.py:63
  122.8 30.0 %select_reduce_fusion.4 = f32[2048,4]{1,0:T(8,128)S(1)} fusion(f32[2048,4,128]{2,1,0:T(4,128)} %gather_fusion, pred[2048]{0:T(1024)(128)(4,1)S(1)} %compare_and_fusion.4, pred[2048,128]{1,0:T(8,128)(4,1)S(1)} %iota_compare_fusion.8), kind=kLoop, calls=%fused_computation.4.clone.1 | loop fusion | flops 3137536 | bytes 4491264 | tf_op jit(solution)/shard_map/while/body/eval_jaxpr/reduce_sum | solution.py:65
  153.9 17.5 %gather_fusion = f32[2048,4,128]{2,1,0:T(4,128)} fusion(f32[2048,4,128]{2,1,0:T(4,128)} %get-tuple-element.449, s32[2048]{0:T(1024)S(1)} %broadcast_clamp_fusion.4), kind=kCustom, calls=%fused_computation.clone.1 | custom fusion | bytes 8396800 | tf_op jit(solution)/shard_map/while/body/eval_jaxpr/jit(_take)/gather | solution.py:63
  171.8 30.0 %select_reduce_fusion.4 = f32[2048,4]{1,0:T(8,128)S(1)} fusion(f32[2048,4,128]{2,1,0:T(4,128)} %gather_fusion, pred[2048]{0:T(1024)(128)(4,1)S(1)} %compare_and_fusion.4, pred[2048,128]{1,0:T(8,128)(4,1)S(1)} %iota_compare_fusion.8), kind=kLoop, calls=%fused_computation.4.clone.1 | loop fusion | flops 3137536 | bytes 4491264 | tf_op jit(solution)/shard_map/while/body/eval_jaxpr/reduce_sum | solution.py:65
  202.9 17.5 %gather_fusion = f32[2048,4,128]{2,1,0:T(4,128)} fusion(f32[2048,4,128]{2,1,0:T(4,128)} %get-tuple-element.449, s32[2048]{0:T(1024)S(1)} %broadcast_clamp_fusion.4), kind=kCustom, calls=%fused_computation.clone.1 | custom fusion | bytes 8396800 | tf_op jit(solution)/shard_map/while/body/eval_jaxpr/jit(_take)/gather | solution.py:63
  220.8 30.0 %select_reduce_fusion.4 = f32[2048,4]{1,0:T(8,128)S(1)} fusion(f32[2048,4,128]{2,1,0:T(4,128)} %gather_fusion, pred[2048]{0:T(1024)(128)(4,1)S(1)} %compare_and_fusion.4, pred[2048,128]{1,0:T(8,128)(4,1)S(1)} %iota_compare_fusion.8), kind=kLoop, calls=%fused_computation.4.clone.1 | loop fusion | flops 3137536 | bytes 4491264 | tf_op jit(solution)/shard_map/while/body/eval_jaxpr/reduce_sum | solution.py:65
  251.9 17.5 %gather_fusion = f32[2048,4,128]{2,1,0:T(4,128)} fusion(f32[2048,4,128]{2,1,0:T(4,128)} %get-tuple-element.449, s32[2048]{0:T(1024)S(1)} %broadcast_clamp_fusion.4), kind=kCustom, calls=%fused_computation.clone.1 | custom fusion | bytes 8396800 | tf_op jit(solution)/shard_map/while/body/eval_jaxpr/jit(_take)/gather | solution.py:63
  269.8 30.0 %select_reduce_fusion.4 = f32[2048,4]{1,0:T(8,128)S(1)} fusion(f32[2048,4,128]{2,1,0:T(4,128)} %gather_fusion, pred[2048]{0:T(1024)(128)(4,1)S(1)} %compare_and_fusion.4, pred[2048,128]{1,0:T(8,128)(4,1)S(1)} %iota_compare_fusion.8), kind=kLoop, calls=%fused_computation.4.clone.1 | loop fusion | flops 3137536 | bytes 4491264 | tf_op jit(solution)/shard_map/while/body/eval_jaxpr/reduce_sum | solution.py:65
  300.9 17.5 %gather_fusion = f32[2048,4,128]{2,1,0:T(4,128)} fusion(f32[2048,4,128]{2,1,0:T(4,128)} %get-tuple-element.449, s32[2048]{0:T(1024)S(1)} %broadcast_clamp_fusion.4), kind=kCustom, calls=%fused_computation.clone.1 | custom fusion | bytes 8396800 | tf_op jit(solution)/shard_map/while/body/eval_jaxpr/jit(_take)/gather | solution.py:63
  318.8 30.0 %select_reduce_fusion.4 = f32[2048,4]{1,0:T(8,128)S(1)} fusion(f32[2048,4,128]{2,1,0:T(4,128)} %gather_fusion, pred[2048]{0:T(1024)(128)(4,1)S(1)} %compare_and_fusion.4, pred[2048,128]{1,0:T(8,128)(4,1)S(1)} %iota_compare_fusion.8), kind=kLoop, calls=%fused_computation.4.clone.1 | loop fusion | flops 3137536 | bytes 4491264 | tf_op jit(solution)/shard_map/while/body/eval_jaxpr/reduce_sum | solution.py:65
  349.9 17.5 %gather_fusion = f32[2048,4,128]{2,1,0:T(4,128)} fusion(f32[2048,4,128]{2,1,0:T(4,128)} %get-tuple-element.449, s32[2048]{0:T(1024)S(1)} %broadcast_clamp_fusion.4), kind=kCustom, calls=%fused_computation.clone.1 | custom fusion | bytes 8396800 | tf_op jit(solution)/shard_map/while/body/eval_jaxpr/jit(_take)/gather | solution.py:63
  367.8 30.0 %select_reduce_fusion.4 = f32[2048,4]{1,0:T(8,128)S(1)} fusion(f32[2048,4,128]{2,1,0:T(4,128)} %gather_fusion, pred[2048]{0:T(1024)(128)(4,1)S(1)} %compare_and_fusion.4, pred[2048,128]{1,0:T(8,128)(4,1)S(1)} %iota_compare_fusion.8), kind=kLoop, calls=%fused_computation.4.clone.1 | loop fusion | flops 3137536 | bytes 4491264 | tf_op jit(solution)/shard_map/while/body/eval_jaxpr/reduce_sum | solution.py:65
  398.9 17.5 %gather_fusion = f32[2048,4,128]{2,1,0:T(4,128)} fusion(f32[2048,4,128]{2,1,0:T(4,128)} %get-tuple-element.449, s32[2048]{0:T(1024)S(1)} %broadcast_clamp_fusion.4), kind=kCustom, calls=%fused_computation.clone.1 | custom fusion | bytes 8396800 | tf_op jit(solution)/shard_map/while/body/eval_jaxpr/jit(_take)/gather | solution.py:63
  416.8 30.0 %select_reduce_fusion.4 = f32[2048,4]{1,0:T(8,128)S(1)} fusion(f32[2048,4,128]{2,1,0:T(4,128)} %gather_fusion, pred[2048]{0:T(1024)(128)(4,1)S(1)} %compare_and_fusion.4, pred[2048,128]{1,0:T(8,128)(4,1)S(1)} %iota_compare_fusion.8), kind=kLoop, calls=%fused_computation.4.clone.1 | loop fusion | flops 3137536 | bytes 4491264 | tf_op jit(solution)/shard_map/while/body/eval_jaxpr/reduce_sum | solution.py:65
  447.9 5.9 copy.37
  453.8 11.4 %all-to-all-start = ((f32[4,32,512]{2,0,1:T(4,128)}), f32[4,32,512]{2,0,1:T(4,128)S(1)}, u32[]{:S(2)}, u32[]{:S(2)}) async-start(f32[4,32,512]{2,0,1:T(4,128)} %bitcast.13), calls=%async_computation | async-start | bytes 524288 | tf_op jit(solution)/shard_map/all_to_all | solution.py:93
  465.4 10.2 %all-to-all-done = f32[4,32,512]{2,0,1:T(4,128)S(1)} async-done(((f32[4,32,512]{2,0,1:T(4,128)}), f32[4,32,512]{2,0,1:T(4,128)S(1)}, u32[]{:S(2)}, u32[]{:S(2)}) %all-to-all-start) | async-done | bytes 262176 | tf_op jit(solution)/shard_map/all_to_all | solution.py:93
  476.0 91.6 %while.41 = (s32[]{:T(128)}, f32[2,2048,4]{2,1,0:T(8,128)S(1)}, s32[2,2048]{1,0:T(2,128)S(1)}, f32[128,4,128]{2,1,0:T(4,128)S(1)}, s32[]{:T(128)}) while((s32[]{:T(128)}, f32[2,2048,4]{2,1,0:T(8,128)S(1)}, s32[2,2048]{1,0:T(2,128)S(1)}, f32[128,4,128]{2,1,0:T(4,128)S(1)}, s32[]{:T(128)}) %tuple.115), condition=%wide.region_5.6_spmd, body=%wide.region_3.5_spmd.sunk | while | flops 3504130 | bytes 15323205 | solution.py:71
  476.0 15.3 %gather_fusion.1 = f32[2048,4,128]{2,1,0:T(4,128)} fusion(f32[128,4,128]{2,1,0:T(4,128)S(1)} %get-tuple-element.464, s32[2048]{0:T(1024)S(1)} %broadcast_clamp_fusion.5), kind=kCustom, calls=%fused_computation.1.clone.1 | custom fusion | bytes 8396800 | tf_op jit(solution)/shard_map/while/body/eval_jaxpr/jit(_take)/gather | solution.py:63
  491.7 30.0 %select_reduce_fusion.5 = f32[2048,4]{1,0:T(8,128)S(1)} fusion(f32[2048,4,128]{2,1,0:T(4,128)} %gather_fusion.1, pred[2048]{0:T(1024)(128)(4,1)S(1)} %compare_and_fusion.5, pred[2048,128]{1,0:T(8,128)(4,1)S(1)} %iota_compare_fusion.9), kind=kLoop, calls=%fused_computation.25.clone.1 | loop fusion | flops 3137536 | bytes 4491264 | tf_op jit(solution)/shard_map/while/body/eval_jaxpr/reduce_sum | solution.py:65
  521.9 15.3 %gather_fusion.1 = f32[2048,4,128]{2,1,0:T(4,128)} fusion(f32[128,4,128]{2,1,0:T(4,128)S(1)} %get-tuple-element.464, s32[2048]{0:T(1024)S(1)} %broadcast_clamp_fusion.5), kind=kCustom, calls=%fused_computation.1.clone.1 | custom fusion | bytes 8396800 | tf_op jit(solution)/shard_map/while/body/eval_jaxpr/jit(_take)/gather | solution.py:63
  537.5 30.0 %select_reduce_fusion.5 = f32[2048,4]{1,0:T(8,128)S(1)} fusion(f32[2048,4,128]{2,1,0:T(4,128)} %gather_fusion.1, pred[2048]{0:T(1024)(128)(4,1)S(1)} %compare_and_fusion.5, pred[2048,128]{1,0:T(8,128)(4,1)S(1)} %iota_compare_fusion.9), kind=kLoop, calls=%fused_computation.25.clone.1 | loop fusion | flops 3137536 | bytes 4491264 | tf_op jit(solution)/shard_map/while/body/eval_jaxpr/reduce_sum | solution.py:65
  569.2 5.1 all-gather.1
  579.6 25.5 %scatter_custom_fusion = f32[128,128]{1,0:T(8,128)} fusion(s32[4096]{0:T(1024)S(1)} %bitcast.117, f32[]{:T(128)} %constant.241.clone.1, f32[4096]{0:T(1024)S(1)} %bitcast.111, s32[4096]{0:T(1024)S(1)} %add_select_fusion.6), kind=kCustom, calls=%fused_computation.71 | custom fusion | flops 1572864 | bytes 99328 | tf_op jit(solution)/shard_map/scatter-add | solution.py:81
  607.7 7.4 %all-to-all-done.1 = f32[32,1,512]{2,1,0:T(1,128)S(1)} async-done(((f32[32,1,512]{2,1,0:T(1,128)}), f32[32,1,512]{2,1,0:T(1,128)S(1)}, u32[]{:S(2)}, u32[]{:S(2)}) %all-to-all-start.1) | async-done | bytes 65568 | tf_op jit(solution)/shard_map/all_to_all | solution.py:117
  615.1 98.8 %scatter_custom_fusion.1 = f32[2048,128]{1,0:T(8,128)} fusion(s32[16384]{0:T(1024)S(1)} %bitcast.112, f32[]{:T(128)} %constant.241.clone.1, f32[16384]{0:T(1024)S(1)} %bitcast.105, s32[16384]{0:T(1024)S(1)} %add_select_fusion.5), kind=kCustom, calls=%fused_computation.50 | custom fusion | flops 6291456 | bytes 1180672 | tf_op jit(solution)/shard_map/scatter-add | solution.py:81
  (185 shorter events, 55.8 us)
Async XLA Ops:
  1.7 16.0 %collective-permute-start.1 = (f32[4,1,16,1024]{3,2,1,0:T(8,128)S(1)}, f32[4,1,16,1024]{3,2,1,0:T(8,128)S(1)}, u32[]{:S(2)}, u32[]{:S(2)}) collective-permute-start(f32[4,1,16,1024]{3,2,1,0:T(8,128)S(1)} %get-tuple-element.310), channel_id=1, source_target_pairs={{0,4},{4,8},{8,12},{12,16},{16,20},{20,24},{24,28},{1,5},{5,9},{9,... | collective-permute-start | bytes 786440 | tf_op jit(solution)/shard_map/ppermute | solution.py:19
  6.6 13.7 %collective-permute-start = (f32[4,1,16,1024]{3,2,1,0:T(8,128)S(1)}, f32[4,1,16,1024]{3,2,1,0:T(8,128)S(1)}, u32[]{:S(2)}, u32[]{:S(2)}) collective-permute-start(f32[4,1,16,1024]{3,2,1,0:T(8,128)S(1)} %get-tuple-element.309), channel_id=1, source_target_pairs={{4,0},{8,4},{12,8},{16,12},{20,16},{24,20},{28,24},{5,1},{9,5},{13... | collective-permute-start | bytes 786440 | tf_op jit(solution)/shard_map/ppermute | solution.py:21
  17.7 10.3 %copy-start.2 = (s32[1,32,512]{2,1,0:T(8,128)S(1)}, s32[1,32,512]{2,1,0:T(8,128)}, u32[]{:S(2)}) copy-start(s32[1,32,512]{2,1,0:T(8,128)} %param.16) | copy-start | bytes 196612
  17.8 10.3 %copy-start.4 = (s32[16,256]{1,0:T(8,128)S(1)}, s32[16,256]{1,0:T(8,128)}, u32[]{:S(2)}) copy-start(s32[16,256]{1,0:T(8,128)} %param.17) | copy-start | bytes 49156
  20.3 9.0 %copy-start.1 = (f32[16,16,1024]{2,1,0:T(8,128)S(1)}, f32[16,16,1024]{2,1,0:T(8,128)}, u32[]{:S(2)}) copy-start(f32[16,16,1024]{2,1,0:T(8,128)} %param.13) | copy-start | bytes 3145732
  20.3 2.2 copy-start
  23.2 4.9 collective-permute-start.2
  24.6 4.4 collective-permute-start.3
  453.8 21.8 %all-to-all-start = ((f32[4,32,512]{2,0,1:T(4,128)}), f32[4,32,512]{2,0,1:T(4,128)S(1)}, u32[]{:S(2)}, u32[]{:S(2)}) async-start(f32[4,32,512]{2,0,1:T(4,128)} %bitcast.13), calls=%async_computation | async-start | bytes 524288 | tf_op jit(solution)/shard_map/all_to_all | solution.py:93
  475.9 92.5 %copy-start.5 = (f32[16,256]{1,0:T(8,128)S(1)}, f32[16,256]{1,0:T(8,128)}, u32[]{:S(2)}) copy-start(f32[16,256]{1,0:T(8,128)} %param.15) | copy-start | bytes 49156
  475.9 103.6 %copy-start.6 = (f32[256]{0:T(256)S(1)}, f32[256]{0:T(256)}, u32[]{:S(2)}) copy-start(f32[256]{0:T(256)} %param.14) | copy-start | bytes 3076
  579.6 136.6 %copy-start.3 = (f32[16,256]{1,0:T(8,128)}, f32[16,256]{1,0:T(8,128)S(1)}, u32[]{:S(2)}) copy-start(f32[16,256]{1,0:T(8,128)S(1)} %multiply_add_fusion) | copy-start | bytes 49156
  605.1 10.0 %all-to-all-start.1 = ((f32[32,1,512]{2,1,0:T(1,128)}), f32[32,1,512]{2,1,0:T(1,128)S(1)}, u32[]{:S(2)}, u32[]{:S(2)}) async-start(f32[32,1,512]{2,1,0:T(1,128)} %bitcast.20), calls=%async_computation.1 | async-start | bytes 131072 | tf_op jit(solution)/shard_map/all_to_all | solution.py:117
  615.1 105.1 %slice-start = ((f32[4,16,16,1024]{3,2,1,0:T(8,128)}), f32[3,16,16,1024]{3,2,1,0:T(8,128)S(1)}, s32[]{:S(2)}) async-start(f32[4,16,16,1024]{3,2,1,0:T(8,128)} %fusion.10), calls=%async_computation.2 | async-start | bytes 6291456 | tf_op jit(solution)/shard_map/slice | solution.py:120
where the time goes:
time: 724 us; the launch traced here: 723 us
  other arithmetic  450 us (62%)
  local copies, waits for them, and re-layouts  209 us (29%)
  waiting for transfers between devices  27.1 us (4%)
  starting transfers between devices  24.4 us (3%)
  blocking collectives  10.1 us (1%)
    reduce_sum x10, other arithmetic, pick_block(): return jnp.sum(jnp.where(chosen[:, None, :], fetched, 0.0), axis=2)  300 us
    gather x10, local copies, waits for them, and re-layouts, pick_block(): fetched = jnp.take(lane_rows, index // LANE_WIDTH, axis=0)  171 us
    scatter-add x2, other arithmetic, place_cells(): return lines.at[index // LANE_WIDTH].add(spread).reshape(total)  124 us
  transfers between devices with their start and end apart: 6, of which 4 were waited for; matrix products, arithmetic and copies ran while one was open for 1% of the time, Pallas kernels for 0%

commit v1 on v0

v1 whole, which is shorter than its diff:
```python
import functools

import jax
import jax.numpy as jnp
from jax import lax
from jax.experimental import pallas as pl
from jax.experimental.pallas import tpu as pltpu
from jax.sharding import PartitionSpec as P

DEPOSIT_SCALE = 2.0
LANES = 128
BF16 = jnp.bfloat16
F32 = jnp.float32
VMEM_LIMIT = 56 * 1024 * 1024


def pieces_of(value, count):
    parts = []
    for _ in range(count):
        part = value.astype(BF16)
        parts.append(part)
        value = value - part.astype(F32)
    return parts


def one_hot(index_row, rows):
    rows_iota = lax.broadcasted_iota(jnp.int32, (rows, index_row.shape[1]), 0)
    return jnp.where(rows_iota == index_row, 1.0, 0.0).astype(BF16)


def halo(state):
    def send(cells, axis, step):
        count = lax.axis_size(axis)
        if step > 0:
            pairs = [(i, i + 1) for i in range(count - 1)]
        else:
            pairs = [(i + 1, i) for i in range(count - 1)]
        return lax.ppermute(cells, axis, pairs)

    x_low = send(state[:, -1], "tile", 1)
    x_high = send(state[:, 0], "tile", -1)
    y_low = send(state[:, :, -1], "seg", 1)
    y_high = send(state[:, :, 0], "seg", -1)
    return x_low, x_high, y_low, y_high


def cell_parts(cells, plane, depth):
    xy = cells // depth
    z = cells % depth
    return (z // LANES) * plane + xy, z % LANES


def serve_kernel(
    state_ref, diff_ref, xl_ref, xh_ref, yl_ref, yh_ref, cells_ref,
    fresh_ref, out_ref, speed_ref, table_ref,
):
    nx, ny, nz = diff_ref.shape
    plane = nx * ny
    chunks = nz // LANES
    step = pl.program_id(0)

    @pl.when(step == 0)
    def _():
        row = lax.broadcasted_iota(jnp.int32, (ny, nz), 0)
        col = lax.broadcasted_iota(jnp.int32, (ny, nz), 1)

        def at_x(x, below, above):
            diffusivity = diff_ref[x]
            speed = None
            for c in range(4):
                cur = state_ref[c, x]
                nbr = above(c) + below(c)
                y_up = jnp.where(row == ny - 1, yh_ref[c, pl.ds(x, 1), :], pltpu.roll(cur, ny - 1, 0))
                y_dn = jnp.where(row == 0, yl_ref[c, pl.ds(x, 1), :], pltpu.roll(cur, 1, 0))
                nbr = nbr + y_up + y_dn
                z_up = jnp.where(col == nz - 1, 0.0, pltpu.roll(cur, nz - 1, 1))
                z_dn = jnp.where(col == 0, 0.0, pltpu.roll(cur, 1, 1))
                nbr = nbr + z_up + z_dn
                new = cur + diffusivity * (nbr - 6.0 * cur)
                fresh_ref[c, x] = new
                if c == 1:
                    speed = new * new
                elif c > 1:
                    speed = speed + new * new
            speed_ref[x] = speed

        at_x(0, lambda c: xl_ref[c], lambda c: state_ref[c, 1])

        def inner(x, carry):
            at_x(x, lambda c: state_ref[c, x - 1], lambda c: state_ref[c, x + 1])
            return carry

        lax.fori_loop(1, nx - 1, inner, 0)
        at_x(nx - 1, lambda c: state_ref[c, nx - 2], lambda c: xh_ref[c])

        for k in range(chunks):
            lanes = slice(k * LANES, (k + 1) * LANES)
            rows = slice(k * plane, (k + 1) * plane)
            for c in range(2):
                source = fresh_ref.at[0] if c == 0 else speed_ref
                block = source[:, :, lanes].reshape(plane, LANES)
                for p, part in enumerate(pieces_of(block.T, 2)):
                    base = (c * 2 + p) * LANES
                    table_ref[base : base + LANES, rows] = part

    where_row, where_lane = cell_parts(cells_ref[0, pl.ds(step, 1), :], plane, nz)
    cap = where_row.shape[1]
    hot = one_hot(where_row, plane * chunks)
    lines = jnp.dot(table_ref[...], hot, preferred_element_type=F32)
    lane_iota = lax.broadcasted_iota(jnp.int32, (LANES, cap), 0)
    chosen = lane_iota == where_lane
    for c in range(2):
        both = lines[2 * c * LANES : (2 * c + 1) * LANES] + lines[(2 * c + 1) * LANES : (2 * c + 2) * LANES]
        out_ref[0, c : c + 1, :] = jnp.sum(jnp.where(chosen, both, 0.0), axis=0, keepdims=True)


def serve(state, diffusivity, halos, wall_cells):
    _, devices, cap = wall_cells.shape
    nx, ny, nz = diffusivity.shape

    def whole(shape):
        return pl.BlockSpec(shape, lambda i: (0,) * len(shape))

    return pl.pallas_call(
        serve_kernel,
        grid=(devices,),
        in_specs=[whole(a.shape) for a in (state, diffusivity, *halos, wall_cells)],
        out_specs=[whole(state.shape), pl.BlockSpec((1, 2, cap), lambda i: (i, 0, 0))],
        out_shape=[
            jax.ShapeDtypeStruct(state.shape, F32),
            jax.ShapeDtypeStruct((devices, 2, cap), F32),
        ],
        scratch_shapes=[
            pltpu.VMEM((nx, ny, nz), F32),
            pltpu.VMEM((4 * LANES, nx * ny * nz // LANES), BF16),
        ],
        compiler_params=pltpu.CompilerParams(vmem_limit_bytes=VMEM_LIMIT),
    )(state, diffusivity, *halos, wall_cells)


def slot_parts(slots, cap, devices):
    owner = slots // cap
    column = slots % cap
    return (column // LANES) * devices + owner, column % LANES


def lookup_kernel(walls_ref, slots_ref, units_ref, gain_ref, shift_ref, ends_ref, table_ref):
    devices, _, cap = walls_ref.shape
    rows, tubes = slots_ref.shape
    chunks = cap // LANES
    slot_rows = devices * chunks
    for k in range(chunks):
        for c in range(2):
            block = walls_ref[:, c, k * LANES : (k + 1) * LANES]
            for p, part in enumerate(pieces_of(block.T, 3)):
                first = p * slot_rows + k * devices
                table_ref[c * LANES : (c + 1) * LANES, first : first + devices] = part
    lane_iota = lax.broadcasted_iota(jnp.int32, (LANES, tubes), 0)
    gain = jnp.ones((1, tubes), F32)
    shift = jnp.zeros((1, tubes), F32)
    for i in range(rows):
        where_row, where_lane = slot_parts(slots_ref[i : i + 1, :], cap, devices)
        hot = one_hot(where_row, slot_rows)
        hot = jnp.concatenate([hot, hot, hot], axis=0)
        lines = jnp.dot(table_ref[...], hot, preferred_element_type=F32)
        chosen = lane_iota == where_lane
        temperature, speed = [
            jnp.sum(jnp.where(chosen, lines[c * LANES : (c + 1) * LANES], 0.0), axis=0, keepdims=True)
            for c in range(2)
        ]
        decay = jnp.exp(-units_ref[i : i + 1, :] * jnp.exp(0.3 * jnp.log(1.0 + speed)))
        source = (1.0 - decay) * temperature
        shift = decay * shift + source
        gain = decay * gain
        gain_ref[i : i + 1, :] = gain
        shift_ref[i : i + 1, :] = shift
    ends_ref[0:1, :] = gain
    ends_ref[1:2, :] = shift


def lookup(walls, slots, units):
    devices, _, cap = walls.shape
    shape = jax.ShapeDtypeStruct(slots.shape, F32)
    return pl.pallas_call(
        lookup_kernel,
        out_shape=[shape, shape, jax.ShapeDtypeStruct((2, slots.shape[1]), F32)],
        scratch_shapes=[pltpu.VMEM((2 * LANES, 3 * devices * cap // LANES), BF16)],
        compiler_params=pltpu.CompilerParams(vmem_limit_bytes=VMEM_LIMIT),
    )(walls, slots, units)


def march_kernel(seg_axis, cap, devices, ends_ref, inlet_ref, gain_ref, shift_ref, slots_ref, enthalpy_ref, out_ref):
    rows, tubes = slots_ref.shape
    chunks = cap // LANES
    slot_rows = devices * chunks
    mine = lax.axis_index(seg_axis)
    start = inlet_ref[...]
    for s in range(ends_ref.shape[0] - 1):
        moved = ends_ref[s, 0:1, :] * start + ends_ref[s, 1:2, :]
        start = jnp.where(s < mine, moved, start)
    enthalpy = gain_ref[...] * start + shift_ref[...]
    enthalpy_ref[...] = enthalpy
    lane_iota = lax.broadcasted_iota(jnp.int32, (LANES, tubes), 0)
    total = jnp.zeros((slot_rows, 3 * LANES), F32)
    before = start
    for i in range(rows):
        after = enthalpy[i : i + 1, :]
        flow = after - before
        before = after
        where_row, where_lane = slot_parts(slots_ref[i : i + 1, :], cap, devices)
        hot = one_hot(where_row, slot_rows)
        chosen = lane_iota == where_lane
        spread = jnp.concatenate(
            [jnp.where(chosen, part.astype(F32), 0.0).astype(BF16) for part in pieces_of(flow, 3)], axis=0
        )
        total = total + lax.dot_general(hot, spread, (((1,), (1,)), ((), ())), preferred_element_type=F32)
    placed = total[:, :LANES] + total[:, LANES : 2 * LANES] + total[:, 2 * LANES :]
    for k in range(chunks):
        out_ref[:, k * LANES : (k + 1) * LANES] = placed[k * devices : (k + 1) * devices]


def march(ends, inlet, gain, shift, slots, cap, devices):
    return pl.pallas_call(
        functools.partial(march_kernel, "seg", cap, devices),
        out_shape=[
            jax.ShapeDtypeStruct(slots.shape, F32),
            jax.ShapeDtypeStruct((devices, cap), F32),
        ],
        compiler_params=pltpu.CompilerParams(vmem_limit_bytes=VMEM_LIMIT),
    )(ends, inlet[None], gain, shift, slots)


def deposit_kernel(flow_ref, cells_ref, fresh_ref, out_ref, total_ref):
    _, nx, ny, nz = fresh_ref.shape
    plane = nx * ny
    chunks = nz // LANES
    step = pl.program_id(0)
    where_row, where_lane = cell_parts(cells_ref[0, pl.ds(step, 1), :], plane, nz)
    cap = where_row.shape[1]
    hot = one_hot(where_row, plane * chunks)
    lane_iota = lax.broadcasted_iota(jnp.int32, (LANES, cap), 0)
    chosen = lane_iota == where_lane
    flow = flow_ref[pl.ds(step, 1), :]
    spread = jnp.concatenate(
        [jnp.where(chosen, part.astype(F32), 0.0).astype(BF16) for part in pieces_of(flow, 2)], axis=0
    )
    added = lax.dot_general(hot, spread, (((1,), (1,)), ((), ())), preferred_element_type=F32)

    @pl.when(step == 0)
    def _():
        total_ref[...] = added

    @pl.when(step > 0)
    def _():
        total_ref[...] += added

    @pl.when(step == pl.num_programs(0) - 1)
    def _():
        for k in range(chunks):
            lanes = slice(k * LANES, (k + 1) * LANES)
            rows = slice(k * plane, (k + 1) * plane)
            deposit = total_ref[rows, :LANES] + total_ref[rows, LANES:]
            out_ref[0, :, :, lanes] = fresh_ref[0, :, :, lanes] - DEPOSIT_SCALE * deposit.reshape(nx, ny, LANES)


def deposit(flow, wall_cells, fresh):
    devices, cap = flow.shape
    _, nx, ny, nz = fresh.shape
    block = pl.BlockSpec((1, nx, ny, nz), lambda i: (0, 0, 0, 0))
    return pl.pallas_call(
        deposit_kernel,
        grid=(devices,),
        in_specs=[
            pl.BlockSpec(flow.shape, lambda i: (0, 0)),
            pl.BlockSpec(wall_cells.shape, lambda i: (0, 0, 0)),
            block,
        ],
        out_specs=block,
        out_shape=jax.ShapeDtypeStruct(fresh.shape, F32),
        scratch_shapes=[pltpu.VMEM((nx * ny * nz // LANES, 2 * LANES), F32)],
        input_output_aliases={2: 0},
        compiler_params=pltpu.CompilerParams(vmem_limit_bytes=VMEM_LIMIT),
    )(flow, wall_cells, fresh)


def body(shell_state, diffusivity, inlet_enthalpy, transfer_units, wall_cells, tube_slots):
    _, devices, cap = wall_cells.shape
    fresh, outgoing = serve(shell_state, diffusivity, halo(shell_state), wall_cells)
    walls = lax.all_to_all(outgoing, ("tile", "seg"), split_axis=0, concat_axis=0, tiled=True)
    gain, shift, ends = lookup(walls, tube_slots, transfer_units)
    all_ends = lax.all_gather(ends, "seg")
    enthalpy, outbound = march(all_ends, inlet_enthalpy, gain, shift, tube_slots, cap, devices)
    flow = lax.all_to_all(outbound, ("tile", "seg"), split_axis=0, concat_axis=0, tiled=True)
    return deposit(flow, wall_cells, fresh), enthalpy


def solution(mesh):
    in_specs = (
        P(None, "tile", "seg", None),
        P("tile", "seg", None),
        P("tile"),
        P("seg", "tile"),
        P(("tile", "seg"), None, None),
        P("seg", "tile"),
    )
    out_specs = (P(None, "tile", "seg", None), P("seg", "tile"))
    return jax.shard_map(body, mesh=mesh, in_specs=in_specs, out_specs=out_specs, check_vma=False)
```

time: 724 us -> 145 us (0.20)
  other arithmetic: 450 us -> 0 us
  local copies, waits for them, and re-layouts: 209 us -> 6.93 us
  Pallas kernels: 0 us -> 90.4 us
  waiting for transfers between devices: 27.1 us -> 4.46 us
  blocking collectives: 10.1 us -> 32 us
  starting transfers between devices: 24.4 us -> 9.55 us
    reduce_sum x10 -> x0, other arithmetic: 300 us -> none  [pick_block(): return jnp.sum(jnp.where(chosen[:, None, :], fetched, 0.0), axis=2)]
    gather x10 -> x0, local copies, waits for them, and re-layouts: 171 us -> none  [pick_block(): fetched = jnp.take(lane_rows, index // LANE_WIDTH, axis=0)]
    scatter-add x2 -> x0, other arithmetic: 124 us -> none  [place_cells(): return lines.at[index // LANE_WIDTH].add(spread).reshape(total)]
    pallas_call x0 -> x4, Pallas kernels: none -> 90.4 us  [the longest x1 49.7 us: serve(): pl.pallas_call(serve_kernel, grid=(devices,), in_specs=[whole(a.shape) fo...]
    all_to_all x0 -> x2, blocking collectives: none -> 26.2 us  [the longest x1 16.5 us: body(): lax.all_to_all(outgoing, ('tile', 'seg'), split_axis=0, concat_axis=0, ti...]
    all_to_all x2 -> x0, waiting for transfers between devices: 17.6 us -> none  [the longest x1 10.2 us: body(): lax.all_to_all(outgoing, ('tile', 'seg'), split_axis=1, concat_axis=1, ti...]
    add x8 -> x0, other arithmetic: 14.5 us -> none  [the longest x1 14.4 us: diffuse(): return state + diffusivity[None] * (neighbours - 6.0 * state)]
    all_to_all x2 -> x0, starting transfers between devices: 13.9 us -> none  [the longest x1 11.4 us: body(): lax.all_to_all(outgoing, ('tile', 'seg'), split_axis=1, concat_axis=1, ti...]
  transfers between devices with their start and end apart: 6 -> 4, of which waited for: 4 -> 1; matrix products, arithmetic and copies ran while one was open for 1% -> 2% of each run, Pallas kernels for 0% -> 0%
where the time goes in v1:
time: 145 us; the launch traced here: 144 us
  Pallas kernels  90.4 us (62%)
  blocking collectives  32 us (22%)
  starting transfers between devices  9.55 us (7%)
  local copies, waits for them, and re-layouts  6.93 us (5%)
  waiting for transfers between devices  4.46 us (3%)
    pallas_call x1, Pallas kernels, serve(): pl.pallas_call(serve_kernel, grid=(devices,), in_specs=[whole(a.shape) fo...  49.7 us
    pallas_call x1, Pallas kernels, deposit(): pl.pallas_call(deposit_kernel, grid=(devices,), in_specs=[pl.BlockSpec(fl...  34.6 us
    all_to_all x1, blocking collectives, body(): lax.all_to_all(outgoing, ('tile', 'seg'), split_axis=0, concat_axis=0, ti...  16.5 us
    all_to_all x1, blocking collectives, body(): lax.all_to_all(outbound, ('tile', 'seg'), split_axis=0, concat_axis=0, ti...  9.72 us
    ppermute x4, starting transfers between devices, send(): return lax.ppermute(cells, axis, pairs)  9.55 us
    all_gather x1, blocking collectives, body(): all_ends = lax.all_gather(ends, 'seg')  5.78 us
    ppermute x4, waiting for transfers between devices, send(): return lax.ppermute(cells, axis, pairs)  4.46 us
    pallas_call x1, Pallas kernels, lookup(): pl.pallas_call(lookup_kernel, out_shape=[shape, shape, jax.ShapeDtypeStru...  3.59 us
  transfers between devices with their start and end apart: 4, of which 1 were waited for; matrix products, arithmetic and copies ran while one was open for 2% of the time, Pallas kernels for 0%

profile of v1, /device:TPU:0, one launch (start us, length us, event | category | flops | bytes accessed | tf_op | source)
XLA Modules:
  0.0 144.1 jit_solution(18307474115049077795)
XLA Ops:
  0.6 1.1 slice_bitcast_fusion
  1.7 1.3 collective-permute-start.1
  3.0 5.5 %collective-permute-start = (f32[4,16,1024]{2,1,0:T(8,128)S(1)}, f32[4,16,1024]{2,1,0:T(8,128)S(1)}, u32[]{:S(2)}, u32[]{:S(2)}) collective-permute-start(f32[4,16,1024]{2,1,0:T(8,128)S(1)} %get-tuple-element.19), channel_id=1, source_target_pairs={{0,4},{4,8},{8,12},{12,16},{16,20},{20,24},{24,28},{1,5},{5,9},{9,... | collective-permute-start | bytes 786440 | tf_op jit(solution)/shard_map/ppermute | solution.py:38
  8.5 2.7 %fusion = (f32[4,16,1,1024]{3,2,1,0:T(1,128)S(1)}, f32[4,16,1,1024]{3,2,1,0:T(1,128)S(1)}) fusion(f32[4,16,16,1024]{3,2,1,0:T(8,128)} %state_ref.1), kind=kLoop, calls=%fused_computation.5 | loop fusion | bytes 1048576 | tf_op jit(solution)/shard_map/slice | solution.py:43
  11.3 1.5 %collective-permute-start.2 = (f32[4,16,1024]{2,1,0:T(8,128)S(1)}, f32[4,16,1024]{2,1,0:T(8,128)S(1)}, u32[]{:S(2)}, u32[]{:S(2)}) collective-permute-start(f32[4,16,1024]{2,1,0:T(8,128)S(1)} %bitcast.21), channel_id=1, source_target_pairs={{0,1},{1,2},{2,3},{4,5},{5,6},{6,7},{8,9},{9,10},{10,11},{12,13},{... | collective-permute-start | bytes 786440 | tf_op jit(solution)/shard_map/ppermute | solution.py:38
  12.9 1.3 collective-permute-start.3
  14.2 0.0 collective-permute-done.1.xh_ref
  14.2 0.0 copy-start
  14.2 4.4 %collective-permute-done.xl_ref = f32[4,16,1024]{2,1,0:T(8,128)S(1)} collective-permute-done((f32[4,16,1024]{2,1,0:T(8,128)S(1)}, f32[4,16,1024]{2,1,0:T(8,128)S(1)}, u32[]{:S(2)}, u32[]{:S(2)}) %collective-permute-start) | collective-permute-done | bytes 262176 | tf_op jit(solution)/shard_map/ppermute | solution.py:38
  18.6 0.0 copy-start.1
  18.6 0.0 collective-permute-done.2.yl_ref
  18.6 0.0 copy-start.2
  18.6 0.0 collective-permute-done.3.yh_ref
  18.6 0.0 copy-done
  18.6 0.7 copy-done.1
  19.3 0.1 copy-done.2
  19.4 0.0 copy-start.3
  19.4 0.7 copy-done.3
  20.1 49.7 %shard_map.77 = (f32[4,16,16,1024]{3,2,1,0:T(8,128)}, f32[32,2,512]{2,1,0:T(2,128)}) custom-call(f32[4,16,16,1024]{3,2,1,0:T(8,128)} %state_ref.1, f32[16,16,1024]{2,1,0:T(8,128)} %diff_ref.1, f32[4,16,1024]{2,1,0:T(8,128)} %copy-done.1, f32[4,16,1024]{2,1,0:T(8,128)} %copy-done, f32[4,16,1024]{2,1,0:T(8,128)} %copy-done.2, f32[4,16,1024]{2,1,0:T(8,128)} %copy-done.3, ...), custom_call_target="tpu_custom_call" | custom-call | tf_op jit(solution)/shard_map/pallas_call | solution.py:124
  69.8 16.5 %all_to_all.16.walls_ref = f32[32,2,512]{2,1,0:T(2,128)} all-to-all(f32[32,2,512]{2,1,0:T(2,128)} %get-tuple-element.9), channel_id=1, replica_groups=mesh['tile'=8,'seg'=4] {'tile','seg'}, dimensions={0} | all-to-all | bytes 262144 | tf_op jit(solution)/shard_map/all_to_all | solution.py:289
  86.3 3.6 %shard_map.78 = (f32[16,256]{1,0:T(8,128)}, f32[16,256]{1,0:T(8,128)}, f32[2,256]{1,0:T(2,128)}) custom-call(f32[32,2,512]{2,1,0:T(2,128)} %all_to_all.16.walls_ref, s32[16,256]{1,0:T(8,128)} %slots_ref.3, f32[16,256]{1,0:T(8,128)} %units_ref.1), custom_call_target="tpu_custom_call" | custom-call | tf_op jit(solution)/shard_map/pallas_call | solution.py:184
  89.9 5.8 %all-gather.1.ends_ref = f32[4,2,256]{2,1,0:T(2,128)} all-gather(f32[1,2,256]{2,1,0:T(2,128)} %bitcast.24), channel_id=2, replica_groups=mesh['tile'=8,'seg'=4] {'seg'}, dimensions={0}, use_global_device_ids=true | all-gather | bytes 10240 | tf_op jit(solution)/shard_map/all_gather | solution.py:291
  95.7 2.5 %shard_map.79 = (f32[16,256]{1,0:T(8,128)}, f32[32,512]{1,0:T(8,128)}) custom-call(f32[4,2,256]{2,1,0:T(2,128)} %all-gather.1.ends_ref, f32[1,256]{1,0:T(1,128)} %bitcast.25, f32[16,256]{1,0:T(8,128)} %get-tuple-element.11.gain_ref, f32[16,256]{1,0:T(8,128)} %get-tuple-element.12.shift_ref, s32[16,256]{1,0:T(8,128)} %slots_ref.3), custom_call_target="tpu_custom_call" | custom-call | tf_op jit(solution)/shard_map/pallas_call | solution.py:223
  98.2 0.9 copy.17
  99.1 9.7 %all_to_all.17 = f32[32,1,512]{2,1,0:T(1,128)S(1)} all-to-all(f32[32,1,512]{2,1,0:T(1,128)S(1)} %copy.17), channel_id=1, replica_groups=mesh['tile'=8,'seg'=4] {'tile','seg'}, dimensions={0} | all-to-all | bytes 131072 | tf_op jit(solution)/shard_map/all_to_all | solution.py:293
  108.8 0.6 copy.28
  109.5 34.6 %shard_map.80 = f32[4,16,16,1024]{3,2,1,0:T(8,128)} custom-call(f32[32,512]{1,0:T(8,128)} %bitcast.20, s32[1,32,512]{2,1,0:T(8,128)} %cells_ref.3, f32[4,16,16,1024]{3,2,1,0:T(8,128)} %get-tuple-element.14.fresh_ref), custom_call_target="tpu_custom_call", output_to_operand_aliasing={{}: (2, {})} | custom-call | tf_op jit(solution)/shard_map/pallas_call | solution.py:270
  (2 shorter events, 0.1 us)
Async XLA Ops:
  1.7 12.4 %collective-permute-start.1 = (f32[4,16,1024]{2,1,0:T(8,128)S(1)}, f32[4,16,1024]{2,1,0:T(8,128)S(1)}, u32[]{:S(2)}, u32[]{:S(2)}) collective-permute-start(f32[4,16,1024]{2,1,0:T(8,128)S(1)} %get-tuple-element.18), channel_id=1, source_target_pairs={{4,0},{8,4},{12,8},{16,12},{20,16},{24,20},{28,24},{5,1},{9,5},{13... | collective-permute-start | bytes 786440 | tf_op jit(solution)/shard_map/ppermute | solution.py:38
  3.0 15.6 %collective-permute-start = (f32[4,16,1024]{2,1,0:T(8,128)S(1)}, f32[4,16,1024]{2,1,0:T(8,128)S(1)}, u32[]{:S(2)}, u32[]{:S(2)}) collective-permute-start(f32[4,16,1024]{2,1,0:T(8,128)S(1)} %get-tuple-element.19), channel_id=1, source_target_pairs={{0,4},{4,8},{8,12},{12,16},{16,20},{20,24},{24,28},{1,5},{5,9},{9,... | collective-permute-start | bytes 786440 | tf_op jit(solution)/shard_map/ppermute | solution.py:38
  11.3 7.3 %collective-permute-start.2 = (f32[4,16,1024]{2,1,0:T(8,128)S(1)}, f32[4,16,1024]{2,1,0:T(8,128)S(1)}, u32[]{:S(2)}, u32[]{:S(2)}) collective-permute-start(f32[4,16,1024]{2,1,0:T(8,128)S(1)} %bitcast.21), channel_id=1, source_target_pairs={{0,1},{1,2},{2,3},{4,5},{5,6},{6,7},{8,9},{9,10},{10,11},{12,13},{... | collective-permute-start | bytes 786440 | tf_op jit(solution)/shard_map/ppermute | solution.py:38
  12.9 5.8 %collective-permute-start.3 = (f32[4,16,1024]{2,1,0:T(8,128)S(1)}, f32[4,16,1024]{2,1,0:T(8,128)S(1)}, u32[]{:S(2)}, u32[]{:S(2)}) collective-permute-start(f32[4,16,1024]{2,1,0:T(8,128)S(1)} %bitcast.22), channel_id=1, source_target_pairs={{1,0},{2,1},{3,2},{5,4},{6,5},{7,6},{9,8},{10,9},{11,10},{13,12},{... | collective-permute-start | bytes 786440 | tf_op jit(solution)/shard_map/ppermute | solution.py:38
  14.2 4.5 %copy-start = (f32[4,16,1024]{2,1,0:T(8,128)}, f32[4,16,1024]{2,1,0:T(8,128)S(1)}, u32[]{:S(2)}) copy-start(f32[4,16,1024]{2,1,0:T(8,128)S(1)} %collective-permute-done.1.xh_ref) | copy-start | bytes 786436
  18.6 0.7 copy-start.1
  18.6 0.8 copy-start.2
  19.4 0.7 copy-start.3

commit v2 on v1

--- a/solution.py
+++ b/solution.py
@@ -1,5 +1,3 @@
-import functools
-
 import jax
 import jax.numpy as jnp
 from jax import lax
@@ -11,6 +9,7 @@
 LANES = 128
 BF16 = jnp.bfloat16
 F32 = jnp.float32
+MESH = pl.DeviceIdType.MESH
 VMEM_LIMIT = 56 * 1024 * 1024
 
 
@@ -28,20 +27,68 @@
     return jnp.where(rows_iota == index_row, 1.0, 0.0).astype(BF16)
 
 
+def halo_kernel(state_ref, xl_ref, xh_ref, yl_ref, yh_ref, send_sems, recv_sems):
+    tile, seg = lax.axis_index("tile"), lax.axis_index("seg")
+    tiles, segs = lax.axis_size("tile"), lax.axis_size("seg")
+    _, nx, ny, _ = state_ref.shape
+    barrier = pltpu.get_barrier_semaphore()
+    sides = (
+        (tile + 1 < tiles, (tile + 1, seg), state_ref.at[:, nx - 1], xl_ref, xh_ref, 0, 1),
+        (tile > 0, (tile - 1, seg), state_ref.at[:, 0], xh_ref, xl_ref, 1, 0),
+        (seg + 1 < segs, (tile, seg + 1), state_ref.at[:, :, ny - 1], yl_ref, yh_ref, 2, 3),
+        (seg > 0, (tile, seg - 1), state_ref.at[:, :, 0], yh_ref, yl_ref, 3, 2),
+    )
+
+    def copy_of(side):
+        _, device, source, there, _, number, _ = side
+        return pltpu.make_async_remote_copy(
+            src_ref=source,
+            dst_ref=there,
+            send_sem=send_sems.at[number],
+            recv_sem=recv_sems.at[number],
+            device_id=device,
+            device_id_type=MESH,
+        )
+
+    for side in sides:
+
+        @pl.when(side[0])
+        def _():
+            pl.semaphore_signal(barrier, inc=1, device_id=side[1], device_id_type=MESH)
+
+        @pl.when(jnp.logical_not(side[0]))
+        def _():
+            side[4][...] = jnp.zeros_like(side[4])
+
+    pl.semaphore_wait(barrier, sum(side[0].astype(jnp.int32) for side in sides))
+
+    for side in sides:
+
+        @pl.when(side[0])
+        def _():
+            copy_of(side).start()
+
+    for side in sides:
+
+        @pl.when(side[0])
+        def _():
+            copy_of(side).wait_send()
+            pltpu.make_async_copy(side[4], side[4], recv_sems.at[side[6]]).wait()
+
+
 def halo(state):
-    def send(cells, axis, step):
-        count = lax.axis_size(axis)
-        if step > 0:
-            pairs = [(i, i + 1) for i in range(count - 1)]
-        else:
-            pairs = [(i + 1, i) for i in range(count - 1)]
-        return lax.ppermute(cells, axis, pairs)
-
-    x_low = send(state[:, -1], "tile", 1)
-    x_high = send(state[:, 0], "tile", -1)
-    y_low = send(state[:, :, -1], "seg", 1)
-    y_high = send(state[:, :, 0], "seg", -1)
-    return x_low, x_high, y_low, y_high
+    _, nx, ny, nz = state.shape
+    vmem = pl.BlockSpec(memory_space=pltpu.VMEM)
+    return pl.pallas_call(
+        halo_kernel,
+        in_specs=[pl.BlockSpec(memory_space=pl.ANY)],
+        out_specs=[vmem] * 4,
+        out_shape=[jax.ShapeDtypeStruct((4, n, nz), F32) for n in (ny, ny, nx, nx)],
+        scratch_shapes=[pltpu.SemaphoreType.DMA((4,)), pltpu.SemaphoreType.DMA((4,))],
+        compiler_params=pltpu.CompilerParams(
+            collective_id=0, has_side_effects=True, vmem_limit_bytes=VMEM_LIMIT
+        ),
+    )(state)
 
 
 def cell_parts(cells, plane, depth):
@@ -144,17 +191,58 @@
     return (column // LANES) * devices + owner, column % LANES
 
 
-def lookup_kernel(walls_ref, slots_ref, units_ref, gain_ref, shift_ref, ends_ref, table_ref):
+def exchange_kernel(
+    walls_ref, slots_ref, units_ref, inlet_ref, enthalpy_ref, flow_ref,
+    walls_in, ends, outbound, table, gains, shifts, send_sems, recv_sems,
+):
     devices, _, cap = walls_ref.shape
     rows, tubes = slots_ref.shape
     chunks = cap // LANES
     slot_rows = devices * chunks
+    segs = lax.axis_size("seg")
+    tile, seg = lax.axis_index("tile"), lax.axis_index("seg")
+    me = tile * segs + seg
+
+    def device(number):
+        return (number // segs, number % segs)
+
+    def send(source, there, phase, to):
+        pltpu.make_async_remote_copy(
+            src_ref=source,
+            dst_ref=there,
+            send_sem=send_sems.at[phase],
+            recv_sem=recv_sems.at[phase],
+            device_id=to,
+            device_id_type=MESH,
+        ).start()
+
+    def wait_for(ref, sem):
+        pltpu.make_async_copy(ref, ref, sem).wait()
+
+    barrier = pltpu.get_barrier_semaphore()
+
+    def greet(j, carry):
+        pl.semaphore_signal(barrier, inc=1, device_id=device((me + j) % devices), device_id_type=MESH)
+        return carry
+
+    lax.fori_loop(1, devices, greet, 0)
+    walls_in[me] = walls_ref[me]
+    pl.semaphore_wait(barrier, devices - 1)
+
+    def push_walls(j, carry):
+        peer = (me + j) % devices
+        send(walls_ref.at[peer], walls_in.at[me], 0, device(peer))
+        return carry
+
+    lax.fori_loop(1, devices, push_walls, 0)
+    wait_for(walls_in.at[0 : devices - 1], recv_sems.at[0])
+
     for k in range(chunks):
         for c in range(2):
-            block = walls_ref[:, c, k * LANES : (k + 1) * LANES]
+            block = walls_in[:, c, k * LANES : (k + 1) * LANES]
             for p, part in enumerate(pieces_of(block.T, 3)):
                 first = p * slot_rows + k * devices
-                table_ref[c * LANES : (c + 1) * LANES, first : first + devices] = part
+                table[c * LANES : (c + 1) * LANES, first : first + devices] = part
     lane_iota = lax.broadcasted_iota(jnp.int32, (LANES, tubes), 0)
     gain = jnp.ones((1, tubes), F32)
     shift = jnp.zeros((1, tubes), F32)
@@ -162,7 +250,7 @@
         where_row, where_lane = slot_parts(slots_ref[i : i + 1, :], cap, devices)
         hot = one_hot(where_row, slot_rows)
         hot = jnp.concatenate([hot, hot, hot], axis=0)
-        lines = jnp.dot(table_ref[...], hot, preferred_element_type=F32)
+        lines = jnp.dot(table[...], hot, preferred_element_type=F32)
         chosen = lane_iota == where_lane
         temperature, speed = [
             jnp.sum(jnp.where(chosen, lines[c * LANES : (c + 1) * LANES], 0.0), axis=0, keepdims=True)
@@ -172,39 +260,23 @@
         source = (1.0 - decay) * temperature
         shift = decay * shift + source
         gain = decay * gain
-        gain_ref[i : i + 1, :] = gain
-        shift_ref[i : i + 1, :] = shift
-    ends_ref[0:1, :] = gain
-    ends_ref[1:2, :] = shift
-
-
-def lookup(walls, slots, units):
-    devices, _, cap = walls.shape
-    shape = jax.ShapeDtypeStruct(slots.shape, F32)
-    return pl.pallas_call(
-        lookup_kernel,
-        out_shape=[shape, shape, jax.ShapeDtypeStruct((2, slots.shape[1]), F32)],
-        scratch_shapes=[pltpu.VMEM((2 * LANES, 3 * devices * cap // LANES), BF16)],
-        compiler_params=pltpu.CompilerParams(vmem_limit_bytes=VMEM_LIMIT),
-    )(walls, slots, units)
-
-
-def march_kernel(seg_axis, cap, devices, ends_ref, inlet_ref, gain_ref, shift_ref, slots_ref, enthalpy_ref, out_ref):
-    rows, tubes = slots_ref.shape
-    chunks = cap // LANES
-    slot_rows = devices * chunks
-    mine = lax.axis_index(seg_axis)
+        gains[i : i + 1, :] = gain
+        shifts[i : i + 1, :] = shift
+    ends[seg] = jnp.concatenate([gain, shift], axis=0)
+
+    for j in range(1, segs):
+        send(ends.at[seg], ends.at[seg], 1, (tile, (seg + j) % segs))
+    wait_for(ends.at[0 : segs - 1], recv_sems.at[1])
+
     start = inlet_ref[...]
-    for s in range(ends_ref.shape[0] - 1):
-        moved = ends_ref[s, 0:1, :] * start + ends_ref[s, 1:2, :]
-        start = jnp.where(s < mine, moved, start)
-    enthalpy = gain_ref[...] * start + shift_ref[...]
-    enthalpy_ref[...] = enthalpy
-    lane_iota = lax.broadcasted_iota(jnp.int32, (LANES, tubes), 0)
+    for s in range(segs - 1):
+        moved = ends[s, 0:1, :] * start + ends[s, 1:2, :]
+        start = jnp.where(s < seg, moved, start)
     total = jnp.zeros((slot_rows, 3 * LANES), F32)
     before = start
     for i in range(rows):
-        after = enthalpy[i : i + 1, :]
+        after = gains[i : i + 1, :] * start + shifts[i : i + 1, :]
+        enthalpy_ref[i : i + 1, :] = after
         flow = after - before
         before = after
         where_row, where_lane = slot_parts(slots_ref[i : i + 1, :], cap, devices)
@@ -216,18 +288,47 @@
         total = total + lax.dot_general(hot, spread, (((1,), (1,)), ((), ())), preferred_element_type=F32)
     placed = total[:, :LANES] + total[:, LANES : 2 * LANES] + total[:, 2 * LANES :]
     for k in range(chunks):
-        out_ref[:, k * LANES : (k + 1) * LANES] = placed[k * devices : (k + 1) * devices]
-
-
-def march(ends, inlet, gain, shift, slots, cap, devices):
+        outbound[:, 0, k * LANES : (k + 1) * LANES] = placed[k * devices : (k + 1) * devices]
+
+    def push_flow(j, carry):
+        peer = (me + j) % devices
+        send(outbound.at[peer], flow_ref.at[me], 2, device(peer))
+        return carry
+
+    lax.fori_loop(1, devices, push_flow, 0)
+    flow_ref[me] = outbound[me]
+    wait_for(walls_in.at[0 : devices - 1], send_sems.at[0])
+    wait_for(ends.at[0 : segs - 1], send_sems.at[1])
+    wait_for(flow_ref.at[0 : devices - 1], send_sems.at[2])
+    wait_for(flow_ref.at[0 : devices - 1], recv_sems.at[2])
+
+
+def exchange(outgoing, slots, units, inlet):
+    devices, _, cap = outgoing.shape
+    tubes = slots.shape[1]
+    vmem = pl.BlockSpec(memory_space=pltpu.VMEM)
     return pl.pallas_call(
-        functools.partial(march_kernel, "seg", cap, devices),
+        exchange_kernel,
+        in_specs=[vmem] * 4,
+        out_specs=[vmem] * 2,
         out_shape=[
             jax.ShapeDtypeStruct(slots.shape, F32),
-            jax.ShapeDtypeStruct((devices, cap), F32),
+            jax.ShapeDtypeStruct((devices, 1, cap), F32),
         ],
-        compiler_params=pltpu.CompilerParams(vmem_limit_bytes=VMEM_LIMIT),
-    )(ends, inlet[None], gain, shift, slots)
+        scratch_shapes=[
+            pltpu.VMEM((devices, 2, cap), F32),
+            pltpu.VMEM((lax.axis_size("seg"), 2, tubes), F32),
+            pltpu.VMEM((devices, 1, cap), F32),
+            pltpu.VMEM((2 * LANES, 3 * devices * cap // LANES), BF16),
+            pltpu.VMEM(slots.shape, F32),
+            pltpu.VMEM(slots.shape, F32),
+            pltpu.SemaphoreType.DMA((3,)),
+            pltpu.SemaphoreType.DMA((3,)),
+        ],
+        compiler_params=pltpu.CompilerParams(
+            collective_id=1, has_side_effects=True, vmem_limit_bytes=VMEM_LIMIT
+        ),
+    )(outgoing, slots, units, inlet[None])
 
 
 def deposit_kernel(flow_ref, cells_ref, fresh_ref, out_ref, total_ref):
@@ -240,7 +341,7 @@
     hot = one_hot(where_row, plane * chunks)
     lane_iota = lax.broadcasted_iota(jnp.int32, (LANES, cap), 0)
     chosen = lane_iota == where_lane
-    flow = flow_ref[pl.ds(step, 1), :]
+    flow = flow_ref[step]
     spread = jnp.concatenate(
         [jnp.where(chosen, part.astype(F32), 0.0).astype(BF16) for part in pieces_of(flow, 2)], axis=0
     )
@@ -264,14 +365,14 @@
 
 
 def deposit(flow, wall_cells, fresh):
-    devices, cap = flow.shape
+    devices, _, cap = flow.shape
     _, nx, ny, nz = fresh.shape
     block = pl.BlockSpec((1, nx, ny, nz), lambda i: (0, 0, 0, 0))
     return pl.pallas_call(
         deposit_kernel,
         grid=(devices,),
         in_specs=[
-            pl.BlockSpec(flow.shape, lambda i: (0, 0)),
+            pl.BlockSpec(flow.shape, lambda i: (0, 0, 0)),
             pl.BlockSpec(wall_cells.shape, lambda i: (0, 0, 0)),
             block,
         ],
@@ -284,13 +385,8 @@
 
 
 def body(shell_state, diffusivity, inlet_enthalpy, transfer_units, wall_cells, tube_slots):
-    _, devices, cap = wall_cells.shape
     fresh, outgoing = serve(shell_state, diffusivity, halo(shell_state), wall_cells)
-    walls = lax.all_to_all(outgoing, ("tile", "seg"), split_axis=0, concat_axis=0, tiled=True)
-    gain, shift, ends = lookup(walls, tube_slots, transfer_units)
-    all_ends = lax.all_gather(ends, "seg")
-    enthalpy, outbound = march(all_ends, inlet_enthalpy, gain, shift, tube_slots, cap, devices)
-    flow = lax.all_to_all(outbound, ("tile", "seg"), split_axis=0, concat_axis=0, tiled=True)
+    enthalpy, flow = exchange(outgoing, tube_slots, transfer_units, inlet_enthalpy)
     return deposit(flow, wall_cells, fresh), enthalpy
 
 

time: 145 us -> 125 us (0.86)
  Pallas kernels: 90.4 us -> 123 us
  blocking collectives: 32 us -> 0 us
  starting transfers between devices: 9.55 us -> 0 us
  local copies, waits for them, and re-layouts: 6.93 us -> 0.61 us
  waiting for transfers between devices: 4.46 us -> 0 us
    pallas_call x2, Pallas kernels: 6.11 us -> 39.1 us  [the longest x1 22.9 us: exchange(): pl.pallas_call(exchange_kernel, in_specs=[vmem] * 4, out_specs=[vmem] * 2...]
    all_to_all x2 -> x0, blocking collectives: 26.2 us -> none  [the longest x1 16.5 us: body(): lax.all_to_all(outgoing, ('tile', 'seg'), split_axis=0, concat_axis=0, ti...]
    ppermute x4 -> x0, starting transfers between devices: 9.55 us -> none  [send(): return lax.ppermute(cells, axis, pairs)]
    all_gather x1 -> x0, blocking collectives: 5.78 us -> none  [body(): all_ends = lax.all_gather(ends, 'seg')]
    ppermute x4 -> x0, waiting for transfers between devices: 4.46 us -> none  [send(): return lax.ppermute(cells, axis, pairs)]
    slice x1 -> x0, local copies, waits for them, and re-layouts: 2.75 us -> none  [halo(): y_high = send(state[:, :, 0], 'seg', -1)]
    unnamed x11 -> x3, local copies, waits for them, and re-layouts: 2.2 us -> 0.61 us
  transfers between devices with their start and end apart: 4 -> 0, of which waited for: 1 -> 0; matrix products, arithmetic and copies ran while one was open for 2% -> 0% of each run, Pallas kernels for 0% -> 0%
where the time goes in v2:
time: 125 us
  Pallas kernels  123 us (98%)
    pallas_call x1, Pallas kernels, serve(): pl.pallas_call(serve_kernel, grid=(devices,), in_specs=[whole(a.shape) fo...  49.8 us
    pallas_call x1, Pallas kernels, deposit(): pl.pallas_call(deposit_kernel, grid=(devices,), in_specs=[pl.BlockSpec(fl...  34.6 us
    pallas_call x1, Pallas kernels, exchange(): pl.pallas_call(exchange_kernel, in_specs=[vmem] * 4, out_specs=[vmem] * 2...  22.9 us
    pallas_call x1, Pallas kernels, halo(): pl.pallas_call(halo_kernel, in_specs=[pl.BlockSpec(memory_space=pl.ANY)],...  16.2 us

profile of v2, /device:TPU:0, one launch (start us, length us, event | category | flops | bytes accessed | tf_op | source)
XLA Modules:
  0.0 124.7 jit_solution(12621969637590957868)
XLA Ops:
  0.6 16.2 %shard_map.77 = (f32[4,16,1024]{2,1,0:T(8,128)}, f32[4,16,1024]{2,1,0:T(8,128)}, f32[4,16,1024]{2,1,0:T(8,128)}, f32[4,16,1024]{2,1,0:T(8,128)}) custom-call(f32[4,16,16,1024]{3,2,1,0:T(8,128)} %state_ref.3), custom_call_target="tpu_custom_call" | custom-call | tf_op jit(solution)/shard_map/pallas_call | solution.py:82
  16.8 49.8 %shard_map.78 = (f32[4,16,16,1024]{3,2,1,0:T(8,128)}, f32[32,2,512]{2,1,0:T(2,128)}) custom-call(f32[4,16,16,1024]{3,2,1,0:T(8,128)} %state_ref.3, f32[16,16,1024]{2,1,0:T(8,128)} %diff_ref.1, f32[4,16,1024]{2,1,0:T(8,128)} %get-tuple-element.10.xl_ref, f32[4,16,1024]{2,1,0:T(8,128)} %get-tuple-element.11.xh_ref, f32[4,16,1024]{2,1,0:T(8,128)} %get-tuple-element.12.yl_ref, ...), custom_call_target="tpu_custom_call" | custom-call | tf_op jit(solution)/shard_map/pallas_call | solution.py:171
  66.6 22.9 %shard_map.79 = (f32[16,256]{1,0:T(8,128)}, f32[32,1,512]{2,1,0:T(1,128)}) custom-call(f32[32,2,512]{2,1,0:T(2,128)} %get-tuple-element.14.walls_ref, s32[16,256]{1,0:T(8,128)} %slots_ref.1, f32[16,256]{1,0:T(8,128)} %units_ref.1, f32[1,256]{1,0:T(1,128)} %bitcast.1), custom_call_target="tpu_custom_call" | custom-call | tf_op jit(solution)/shard_map/pallas_call | solution.py:310
  89.5 0.0 copy-start
  89.5 34.6 %shard_map.80 = f32[4,16,16,1024]{3,2,1,0:T(8,128)} custom-call(f32[32,1,512]{2,1,0:T(1,128)} %get-tuple-element.15.flow_ref, s32[1,32,512]{2,1,0:T(8,128)} %cells_ref.3, f32[4,16,16,1024]{3,2,1,0:T(8,128)} %get-tuple-element.16.fresh_ref), custom_call_target="tpu_custom_call", output_to_operand_aliasing={{}: (2, {})} | custom-call | tf_op jit(solution)/shard_map/pallas_call | solution.py:371
  124.1 0.0 copy-done
  124.1 0.6 copy.11
Async XLA Ops:
  89.5 34.6 %copy-start = (f32[16,256]{1,0:T(8,128)S(1)}, f32[16,256]{1,0:T(8,128)}, u32[]{:S(2)}) copy-start(f32[16,256]{1,0:T(8,128)} %get-tuple-element.21) | copy-start | bytes 49156

commit v3 on v1

v3 whole, which is shorter than its diff:
```python
import jax
import jax.numpy as jnp
from jax import lax
from jax.experimental import pallas as pl
from jax.experimental.pallas import tpu as pltpu
from jax.sharding import PartitionSpec as P

DEPOSIT_SCALE = 2.0
LANES = 128
GROUP = 4
BF16 = jnp.bfloat16
F32 = jnp.float32
MESH = pl.DeviceIdType.MESH
VMEM_LIMIT = 56 * 1024 * 1024


def pieces_of(value, count):
    parts = []
    for _ in range(count):
        part = value.astype(BF16)
        parts.append(part)
        value = value - part.astype(F32)
    return parts


def one_hot(index_row, rows):
    narrow = jnp.int16 if rows <= 32768 else jnp.int32
    rows_iota = lax.broadcasted_iota(jnp.int32, (rows, index_row.shape[1]), 0).astype(narrow)
    return jnp.where(rows_iota == index_row.astype(narrow), jnp.ones((), BF16), jnp.zeros((), BF16))


def cell_parts(cells, plane, depth):
    xy = cells // depth
    z = cells % depth
    return (z // LANES) * plane + xy, z % LANES


def slot_parts(slots, cap, devices):
    owner = slots // cap
    column = slots % cap
    return (column // LANES) * devices + owner, column % LANES


def march_kernel(
    state_ref, diff_ref, cells_ref, slots_ref, units_ref, inlet_ref,
    fresh_ref, enthalpy_ref, flow_ref,
    x_low, x_high, y_low, y_high, y_first, y_last, speed_field, cell_table,
    outgoing, walls_in, ends, outbound, flow_in, slot_table, gains, shifts,
    halo_send, halo_recv, send_sems, recv_sems,
):
    nx, ny, nz = diff_ref.shape
    plane = nx * ny
    step = pl.program_id(0)
    _, devices, cap = cells_ref.shape
    rows, tubes = slots_ref.shape
    slot_rows = devices * cap // LANES
    tiles, segs = lax.axis_size("tile"), lax.axis_size("seg")
    tile, seg = lax.axis_index("tile"), lax.axis_index("seg")
    me = tile * segs + seg
    peer = (me + step) % devices

    def device(number):
        return (number // segs, number % segs)

    def copy_of(source, there, send_sem, recv_sem, to):
        return pltpu.make_async_remote_copy(
            src_ref=source, dst_ref=there, send_sem=send_sem, recv_sem=recv_sem,
            device_id=to, device_id_type=MESH,
        )

    def send(source, there, phase, to):
        copy_of(source, there, send_sems.at[phase], recv_sems.at[phase], to).start()

    def wait_for(ref, sem):
        pltpu.make_async_copy(ref, ref, sem).wait()

    @pl.when(step == 0)
    def _():
        barrier = pltpu.get_barrier_semaphore()

        def greet(j, carry):
            pl.semaphore_signal(barrier, inc=1, device_id=device((me + j) % devices), device_id_type=MESH)
            return carry

        lax.fori_loop(1, devices, greet, 0)
        for c in range(4):
            for x in range(nx):
                y_first[c, x : x + 1, :] = state_ref[c, x, 0:1, :]
                y_last[c, x : x + 1, :] = state_ref[c, x, ny - 1 : ny, :]
        sides = (
            (tile + 1 < tiles, (tile + 1, seg), state_ref.at[:, nx - 1], x_low, x_high, 0, 1),
            (tile > 0, (tile - 1, seg), state_ref.at[:, 0], x_high, x_low, 1, 0),
            (seg + 1 < segs, (tile, seg + 1), y_last, y_low, y_high, 2, 3),
            (seg > 0, (tile, seg - 1), y_first, y_high, y_low, 3, 2),
        )
        pl.semaphore_wait(barrier, devices - 1)
        for side in sides:

            @pl.when(side[0])
            def _():
                copy_of(side[2], side[3], halo_send.at[side[5]], halo_recv.at[side[5]], side[1]).start()

            @pl.when(jnp.logical_not(side[0]))
            def _():
                side[4][...] = jnp.zeros_like(side[4])

        for side in sides:

            @pl.when(side[0])
            def _():
                wait_for(side[4], halo_recv.at[side[6]])
                wait_for(side[4], halo_send.at[side[5]])

        chunks = nz // LANES
        row = lax.broadcasted_iota(jnp.int32, (ny, nz), 0)
        col = lax.broadcasted_iota(jnp.int32, (ny, nz), 1)

        def at_x(x, below, above):
            diffusivity = diff_ref[x]
            speed = None
            for c in range(4):
                cur = state_ref[c, x]
                nbr = above(c) + below(c)
                y_up = jnp.where(row == ny - 1, y_high[c, pl.ds(x, 1), :], pltpu.roll(cur, ny - 1, 0))
                y_dn = jnp.where(row == 0, y_low[c, pl.ds(x, 1), :], pltpu.roll(cur, 1, 0))
                nbr = nbr + y_up + y_dn
                z_up = jnp.where(col == nz - 1, 0.0, pltpu.roll(cur, nz - 1, 1))
                z_dn = jnp.where(col == 0, 0.0, pltpu.roll(cur, 1, 1))
                nbr = nbr + z_up + z_dn
                new = cur + diffusivity * (nbr - 6.0 * cur)
                fresh_ref[c, x] = new
                if c == 1:
                    speed = new * new
                elif c > 1:
                    speed = speed + new * new
            speed_field[x] = speed

        at_x(0, lambda c: x_low[c], lambda c: state_ref[c, 1])

        def inner(x, carry):
            at_x(x, lambda c: state_ref[c, x - 1], lambda c: state_ref[c, x + 1])
            return carry

        lax.fori_loop(1, nx - 1, inner, 0)
        at_x(nx - 1, lambda c: state_ref[c, nx - 2], lambda c: x_high[c])

        for k in range(chunks):
            lanes = slice(k * LANES, (k + 1) * LANES)
            rows = slice(k * plane, (k + 1) * plane)
            for c in range(2):
                source = fresh_ref.at[0] if c == 0 else speed_field
                block = source[:, :, lanes].reshape(plane, LANES)
                for p, part in enumerate(pieces_of(block.T, 2)):
                    base = (c * 2 + p) * LANES
                    cell_table[base : base + LANES, rows] = part

    where_row, where_lane = cell_parts(cells_ref[0, pl.ds(peer, 1), :], plane, nz)
    hot = one_hot(where_row, plane * (nz // LANES))
    lines = jnp.dot(cell_table[...], hot, preferred_element_type=F32)
    chosen = lax.broadcasted_iota(jnp.int32, (LANES, cap), 0) == where_lane
    picked = []
    for c in range(2):
        both = lines[2 * c * LANES : (2 * c + 1) * LANES] + lines[(2 * c + 1) * LANES : (2 * c + 2) * LANES]
        picked.append(jnp.sum(jnp.where(chosen, both, 0.0), axis=0, keepdims=True))
    picked = jnp.concatenate(picked, axis=0)

    @pl.when(step == 0)
    def _():
        walls_in[me] = picked

    @pl.when(step > 0)
    def _():
        outgoing[peer] = picked
        send(outgoing.at[peer], walls_in.at[me], 0, device(peer))

    @pl.when(step == devices - 1)
    def _():
        chunks = cap // LANES
        wait_for(walls_in.at[0 : devices - 1], recv_sems.at[0])
        for k in range(chunks):
            for c in range(2):
                block = walls_in[:, c, k * LANES : (k + 1) * LANES]
                for p, part in enumerate(pieces_of(block.T, 3)):
                    first = p * slot_rows + k * devices
                    slot_table[c * LANES : (c + 1) * LANES, first : first + devices] = part
        lane_iota = lax.broadcasted_iota(jnp.int32, (LANES, tubes), 0)
        gain = jnp.ones((1, tubes), F32)
        shift = jnp.zeros((1, tubes), F32)
        for i in range(rows):
            where_row, where_lane = slot_parts(slots_ref[i : i + 1, :], cap, devices)
            hot = one_hot(where_row, slot_rows)
            hot = jnp.concatenate([hot, hot, hot], axis=0)
            lines = jnp.dot(slot_table[...], hot, preferred_element_type=F32)
            chosen = lane_iota == where_lane
            temperature, speed = [
                jnp.sum(jnp.where(chosen, lines[c * LANES : (c + 1) * LANES], 0.0), axis=0, keepdims=True)
                for c in range(2)
            ]
            decay = jnp.exp(-units_ref[i : i + 1, :] * jnp.exp(0.3 * jnp.log(1.0 + speed)))
            source = (1.0 - decay) * temperature
            shift = decay * shift + source
            gain = decay * gain
            gains[i : i + 1, :] = gain
            shifts[i : i + 1, :] = shift
        ends[seg] = jnp.concatenate([gain, shift], axis=0)

        for j in range(1, segs):
            send(ends.at[seg], ends.at[seg], 1, (tile, (seg + j) % segs))
        wait_for(ends.at[0 : segs - 1], recv_sems.at[1])

        start = inlet_ref[...]
        for s in range(segs - 1):
            moved = ends[s, 0:1, :] * start + ends[s, 1:2, :]
            start = jnp.where(s < seg, moved, start)
        total = jnp.zeros((slot_rows, 3 * LANES), F32)
        before = start
        for i in range(rows):
            after = gains[i : i + 1, :] * start + shifts[i : i + 1, :]
            enthalpy_ref[i : i + 1, :] = after
            flow = after - before
            before = after
            where_row, where_lane = slot_parts(slots_ref[i : i + 1, :], cap, devices)
            hot = one_hot(where_row, slot_rows)
            chosen = lane_iota == where_lane
            spread = jnp.concatenate(
                [jnp.where(chosen, part.astype(F32), 0.0).astype(BF16) for part in pieces_of(flow, 3)], axis=0
            )
            total = total + lax.dot_general(hot, spread, (((1,), (1,)), ((), ())), preferred_element_type=F32)
        placed = total[:, :LANES] + total[:, LANES : 2 * LANES] + total[:, 2 * LANES :]
        for k in range(chunks):
            outbound[:, 0, k * LANES : (k + 1) * LANES] = placed[k * devices : (k + 1) * devices]

        def push_flow(j, carry):
            peer = (me + j) % devices
            send(outbound.at[peer], flow_in.at[me], 2, device(peer))
            return carry

        lax.fori_loop(1, devices, push_flow, 0)
        flow_in[me] = outbound[me]
        wait_for(outgoing.at[0 : devices - 1], send_sems.at[0])
        wait_for(ends.at[0 : segs - 1], send_sems.at[1])
        wait_for(outbound.at[0 : devices - 1], send_sems.at[2])
        wait_for(flow_in.at[0 : devices - 1], recv_sems.at[2])
        flow_ref[...] = flow_in[...]


def march(state, diffusivity, wall_cells, slots, units, inlet):
    _, devices, cap = wall_cells.shape
    nx, ny, nz = diffusivity.shape
    rows, tubes = slots.shape
    ins = (state, diffusivity, wall_cells, slots, units, inlet[None])
    outs = (state.shape, slots.shape, (devices, 1, cap))

    def whole(shape):
        return pl.BlockSpec(shape, lambda i: (0,) * len(shape))

    return pl.pallas_call(
        march_kernel,
        grid=(devices,),
        in_specs=[whole(a.shape) for a in ins],
        out_specs=[whole(shape) for shape in outs],
        out_shape=[jax.ShapeDtypeStruct(shape, F32) for shape in outs],
        scratch_shapes=[
            pltpu.VMEM((4, ny, nz), F32),
            pltpu.VMEM((4, ny, nz), F32),
            pltpu.VMEM((4, nx, nz), F32),
            pltpu.VMEM((4, nx, nz), F32),
            pltpu.VMEM((4, nx, nz), F32),
            pltpu.VMEM((4, nx, nz), F32),
            pltpu.VMEM((nx, ny, nz), F32),
            pltpu.VMEM((4 * LANES, nx * ny * nz // LANES), BF16),
            pltpu.VMEM((devices, 2, cap), F32),
            pltpu.VMEM((devices, 2, cap), F32),
            pltpu.VMEM((lax.axis_size("seg"), 2, tubes), F32),
            pltpu.VMEM((devices, 1, cap), F32),
            pltpu.VMEM((devices, 1, cap), F32),
            pltpu.VMEM((2 * LANES, 3 * devices * cap // LANES), BF16),
            pltpu.VMEM((rows, tubes), F32),
            pltpu.VMEM((rows, tubes), F32),
            pltpu.SemaphoreType.DMA((4,)),
            pltpu.SemaphoreType.DMA((4,)),
            pltpu.SemaphoreType.DMA((3,)),
            pltpu.SemaphoreType.DMA((3,)),
        ],
        compiler_params=pltpu.CompilerParams(
            collective_id=0, has_side_effects=True, vmem_limit_bytes=VMEM_LIMIT
        ),
    )(*ins)


def deposit_kernel(flow_ref, cells_ref, fresh_ref, out_ref, total_ref):
    _, nx, ny, nz = fresh_ref.shape
    plane = nx * ny
    chunks = nz // LANES
    step = pl.program_id(0)
    cap = flow_ref.shape[2]
    lane_iota = lax.broadcasted_iota(jnp.int32, (LANES, cap), 0)
    hots, spreads = [], []
    for j in range(GROUP):
        owner = step * GROUP + j
        where_row, where_lane = cell_parts(cells_ref[0, pl.ds(owner, 1), :], plane, nz)
        chosen = lane_iota == where_lane
        parts = [jnp.where(chosen, part.astype(F32), 0.0).astype(BF16) for part in pieces_of(flow_ref[owner], 2)]
        hots.append(one_hot(where_row, plane * chunks))
        spreads.append(jnp.concatenate(parts, axis=0))
    added = lax.dot_general(
        jnp.concatenate(hots, axis=1),
        jnp.concatenate(spreads, axis=1),
        (((1,), (1,)), ((), ())),
        preferred_element_type=F32,
    )

    @pl.when(step == 0)
    def _():
        total_ref[...] = added

    @pl.when(step > 0)
    def _():
        total_ref[...] += added

    @pl.when(step == pl.num_programs(0) - 1)
    def _():
        for k in range(chunks):
            lanes = slice(k * LANES, (k + 1) * LANES)
            rows = slice(k * plane, (k + 1) * plane)
            deposit = total_ref[rows, :LANES] + total_ref[rows, LANES:]
            out_ref[0, :, :, lanes] = fresh_ref[0, :, :, lanes] - DEPOSIT_SCALE * deposit.reshape(nx, ny, LANES)


def deposit(flow, wall_cells, fresh):
    devices, _, cap = flow.shape
    _, nx, ny, nz = fresh.shape
    block = pl.BlockSpec((1, nx, ny, nz), lambda i: (0, 0, 0, 0))
    return pl.pallas_call(
        deposit_kernel,
        grid=(devices // GROUP,),
        in_specs=[
            pl.BlockSpec(flow.shape, lambda i: (0, 0, 0)),
            pl.BlockSpec(wall_cells.shape, lambda i: (0, 0, 0)),
            block,
        ],
        out_specs=block,
        out_shape=jax.ShapeDtypeStruct(fresh.shape, F32),
        scratch_shapes=[pltpu.VMEM((nx * ny * nz // LANES, 2 * LANES), F32)],
        input_output_aliases={2: 0},
        compiler_params=pltpu.CompilerParams(vmem_limit_bytes=VMEM_LIMIT),
    )(flow, wall_cells, fresh)


def body(shell_state, diffusivity, inlet_enthalpy, transfer_units, wall_cells, tube_slots):
    fresh, enthalpy, flow = march(
        shell_state, diffusivity, wall_cells, tube_slots, transfer_units, inlet_enthalpy
    )
    return deposit(flow, wall_cells, fresh), enthalpy


def solution(mesh):
    in_specs = (
        P(None, "tile", "seg", None),
        P("tile", "seg", None),
        P("tile"),
        P("seg", "tile"),
        P(("tile", "seg"), None, None),
        P("seg", "tile"),
    )
    out_specs = (P(None, "tile", "seg", None), P("seg", "tile"))
    return jax.shard_map(body, mesh=mesh, in_specs=in_specs, out_specs=out_specs, check_vma=False)
```

time: 145 us -> 114 us (0.79)
  blocking collectives: 32 us -> 0 us
  Pallas kernels: 90.4 us -> 107 us
  starting transfers between devices: 9.55 us -> 0 us
  waiting for transfers between devices: 4.46 us -> 0 us
  local copies, waits for them, and re-layouts: 6.93 us -> 5.41 us
    all_to_all x2 -> x0, blocking collectives: 26.2 us -> none  [the longest x1 16.5 us: body(): lax.all_to_all(outgoing, ('tile', 'seg'), split_axis=0, concat_axis=0, ti...]
    pallas_call x4 -> x2, Pallas kernels: 90.4 us -> 107 us  [the longest x1 84 us: march(): pl.pallas_call(march_kernel, grid=(devices,), in_specs=[whole(a.shape) fo...]
    ppermute x4 -> x0, starting transfers between devices: 9.55 us -> none  [send(): return lax.ppermute(cells, axis, pairs)]
    all_gather x1 -> x0, blocking collectives: 5.78 us -> none  [body(): all_ends = lax.all_gather(ends, 'seg')]
    ppermute x4 -> x0, waiting for transfers between devices: 4.46 us -> none  [send(): return lax.ppermute(cells, axis, pairs)]
    unnamed x11 -> x4, local copies, waits for them, and re-layouts: 2.2 us -> 5.41 us
    slice x1 -> x0, local copies, waits for them, and re-layouts: 2.75 us -> none  [halo(): y_high = send(state[:, :, 0], 'seg', -1)]
  transfers between devices with their start and end apart: 4 -> 0, of which waited for: 1 -> 0; matrix products, arithmetic and copies ran while one was open for 2% -> 0% of each run, Pallas kernels for 0% -> 0%
where the time goes in v3:
time: 114 us
  Pallas kernels  107 us (94%)
  local copies, waits for them, and re-layouts  5.41 us (5%)
    pallas_call x1, Pallas kernels, march(): pl.pallas_call(march_kernel, grid=(devices,), in_specs=[whole(a.shape) fo...  84 us
    pallas_call x1, Pallas kernels, deposit(): pl.pallas_call(deposit_kernel, grid=(devices // GROUP,), in_specs=[pl.Blo...  23.5 us
    unnamed x4, local copies, waits for them, and re-layouts  5.41 us

profile of v3, /device:TPU:0, one launch (start us, length us, event | category | flops | bytes accessed | tf_op | source)
XLA Modules:
  0.0 113.5 jit_solution(4555133753656963087)
XLA Ops:
  0.6 84.0 %shard_map.77 = (f32[4,16,16,1024]{3,2,1,0:T(8,128)}, f32[16,256]{1,0:T(8,128)}, f32[32,1,512]{2,1,0:T(1,128)}) custom-call(f32[4,16,16,1024]{3,2,1,0:T(8,128)} %state_ref.1, f32[16,16,1024]{2,1,0:T(8,128)} %diff_ref.1, s32[1,32,512]{2,1,0:T(8,128)} %cells_ref.3, s32[16,256]{1,0:T(8,128)} %slots_ref.1, f32[16,256]{1,0:T(8,128)} %units_ref.1, f32[1,256]{1,0:T(1,128)} %bitcast.1), custom_call_target="tpu_custom_call" | custom-call | tf_op jit(solution)/shard_map/pallas_call | solution.py:257
  84.6 23.5 %shard_map.78 = f32[4,16,16,1024]{3,2,1,0:T(8,128)} custom-call(f32[32,1,512]{2,1,0:T(1,128)} %get-tuple-element.5.flow_ref, s32[1,32,512]{2,1,0:T(8,128)} %cells_ref.3, f32[4,16,16,1024]{3,2,1,0:T(8,128)} %get-tuple-element.6.fresh_ref), custom_call_target="tpu_custom_call", output_to_operand_aliasing={{}: (2, {})} | custom-call | tf_op jit(solution)/shard_map/pallas_call | solution.py:334
  108.1 0.0 copy-start
  108.1 4.8 %copy.12 = f32[4,16,16,1024]{3,2,1,0:T(8,128)} copy(f32[4,16,16,1024]{3,2,1,0:T(8,128)} %shard_map.78) | data formatting | bytes 8388608
  112.9 0.0 copy-done
  112.9 0.6 copy.13
Async XLA Ops:
  108.1 4.8 %copy-start = (f32[16,256]{1,0:T(8,128)S(1)}, f32[16,256]{1,0:T(8,128)}, u32[]{:S(2)}) copy-start(f32[16,256]{1,0:T(8,128)} %get-tuple-element.11) | copy-start | bytes 49156

commit v4 on v3

--- a/solution.py
+++ b/solution.py
@@ -8,6 +8,7 @@
 DEPOSIT_SCALE = 2.0
 LANES = 128
 GROUP = 4
+PAIR = 2
 BF16 = jnp.bfloat16
 F32 = jnp.float32
 MESH = pl.DeviceIdType.MESH
@@ -57,7 +58,7 @@
     tiles, segs = lax.axis_size("tile"), lax.axis_size("seg")
     tile, seg = lax.axis_index("tile"), lax.axis_index("seg")
     me = tile * segs + seg
-    peer = (me + step) % devices
+    peers = [(me + step * PAIR + u) % devices for u in range(PAIR)]
 
     def device(number):
         return (number // segs, number % segs)
@@ -154,26 +155,32 @@
                     base = (c * 2 + p) * LANES
                     cell_table[base : base + LANES, rows] = part
 
-    where_row, where_lane = cell_parts(cells_ref[0, pl.ds(peer, 1), :], plane, nz)
-    hot = one_hot(where_row, plane * (nz // LANES))
-    lines = jnp.dot(cell_table[...], hot, preferred_element_type=F32)
-    chosen = lax.broadcasted_iota(jnp.int32, (LANES, cap), 0) == where_lane
-    picked = []
-    for c in range(2):
-        both = lines[2 * c * LANES : (2 * c + 1) * LANES] + lines[(2 * c + 1) * LANES : (2 * c + 2) * LANES]
-        picked.append(jnp.sum(jnp.where(chosen, both, 0.0), axis=0, keepdims=True))
-    picked = jnp.concatenate(picked, axis=0)
+    blocks = []
+    for peer in peers:
+        where_row, where_lane = cell_parts(cells_ref[0, pl.ds(peer, 1), :], plane, nz)
+        hot = one_hot(where_row, plane * (nz // LANES))
+        lines = jnp.dot(cell_table[...], hot, preferred_element_type=F32)
+        chosen = lax.broadcasted_iota(jnp.int32, (LANES, cap), 0) == where_lane
+        picked = []
+        for c in range(2):
+            both = lines[2 * c * LANES : (2 * c + 1) * LANES] + lines[(2 * c + 1) * LANES : (2 * c + 2) * LANES]
+            picked.append(jnp.sum(jnp.where(chosen, both, 0.0), axis=0, keepdims=True))
+        blocks.append(jnp.concatenate(picked, axis=0))
 
     @pl.when(step == 0)
     def _():
-        walls_in[me] = picked
+        walls_in[me] = blocks[0]
 
     @pl.when(step > 0)
     def _():
-        outgoing[peer] = picked
+        outgoing[peers[0]] = blocks[0]
+        send(outgoing.at[peers[0]], walls_in.at[me], 0, device(peers[0]))
+
+    for peer, block in zip(peers[1:], blocks[1:]):
+        outgoing[peer] = block
         send(outgoing.at[peer], walls_in.at[me], 0, device(peer))
 
-    @pl.when(step == devices - 1)
+    @pl.when(step == devices // PAIR - 1)
     def _():
         chunks = cap // LANES
         wait_for(walls_in.at[0 : devices - 1], recv_sems.at[0])
@@ -256,7 +263,7 @@
 
     return pl.pallas_call(
         march_kernel,
-        grid=(devices,),
+        grid=(devices // PAIR,),
         in_specs=[whole(a.shape) for a in ins],
         out_specs=[whole(shape) for shape in outs],
         out_shape=[jax.ShapeDtypeStruct(shape, F32) for shape in outs],
@@ -288,11 +295,16 @@
     )(*ins)
 
 
-def deposit_kernel(flow_ref, cells_ref, fresh_ref, out_ref, total_ref):
+def deposit_kernel(flow_ref, cells_ref, fresh_ref, rest_ref, out_ref, total_ref, heated_ref, sems):
     _, nx, ny, nz = fresh_ref.shape
+    keep = pltpu.make_async_copy(rest_ref.at[1:4], out_ref.at[1:4], sems.at[0])
     plane = nx * ny
     chunks = nz // LANES
     step = pl.program_id(0)
+    @pl.when(step == 0)
+    def _():
+        keep.start()
+
     cap = flow_ref.shape[2]
     lane_iota = lax.broadcasted_iota(jnp.int32, (LANES, cap), 0)
     hots, spreads = [], []
@@ -324,7 +336,11 @@
             lanes = slice(k * LANES, (k + 1) * LANES)
             rows = slice(k * plane, (k + 1) * plane)
             deposit = total_ref[rows, :LANES] + total_ref[rows, LANES:]
-            out_ref[0, :, :, lanes] = fresh_ref[0, :, :, lanes] - DEPOSIT_SCALE * deposit.reshape(nx, ny, LANES)
+            heated_ref[:, :, lanes] = fresh_ref[0, :, :, lanes] - DEPOSIT_SCALE * deposit.reshape(nx, ny, LANES)
+        give = pltpu.make_async_copy(heated_ref, out_ref.at[0], sems.at[1])
+        give.start()
+        give.wait()
+        keep.wait()
 
 
 def deposit(flow, wall_cells, fresh):
@@ -338,13 +354,17 @@
             pl.BlockSpec(flow.shape, lambda i: (0, 0, 0)),
             pl.BlockSpec(wall_cells.shape, lambda i: (0, 0, 0)),
             block,
+            pl.BlockSpec(memory_space=pl.ANY),
         ],
-        out_specs=block,
+        out_specs=pl.BlockSpec(memory_space=pl.ANY),
         out_shape=jax.ShapeDtypeStruct(fresh.shape, F32),
-        scratch_shapes=[pltpu.VMEM((nx * ny * nz // LANES, 2 * LANES), F32)],
-        input_output_aliases={2: 0},
+        scratch_shapes=[
+            pltpu.VMEM((nx * ny * nz // LANES, 2 * LANES), F32),
+            pltpu.VMEM((nx, ny, nz), F32),
+            pltpu.SemaphoreType.DMA((2,)),
+        ],
         compiler_params=pltpu.CompilerParams(vmem_limit_bytes=VMEM_LIMIT),
-    )(flow, wall_cells, fresh)
+    )(flow, wall_cells, fresh, fresh)
 
 
 def body(shell_state, diffusivity, inlet_enthalpy, transfer_units, wall_cells, tube_slots):

time: 114 us -> 180 us (1.58)
  Pallas kernels: 107 us -> 179 us
  local copies, waits for them, and re-layouts: 5.41 us -> 0.61 us
    pallas_call x1, Pallas kernels: 23.5 us -> 97.7 us  [deposit(): pl.pallas_call(deposit_kernel, grid=(devices // GROUP,), in_specs=[pl.Blo...]
    unnamed x4 -> x3, local copies, waits for them, and re-layouts: 5.41 us -> 0.61 us
    pallas_call x1, Pallas kernels: 84 us -> 81.2 us  [march(): pl.pallas_call(march_kernel, grid=(devices // PAIR,), in_specs=[whole(a.s...]
where the time goes in v4:
time: 180 us
  Pallas kernels  179 us (99%)
    pallas_call x1, Pallas kernels, deposit(): pl.pallas_call(deposit_kernel, grid=(devices // GROUP,), in_specs=[pl.Blo...  97.7 us
    pallas_call x1, Pallas kernels, march(): pl.pallas_call(march_kernel, grid=(devices // PAIR,), in_specs=[whole(a.s...  81.2 us

profile of v4, /device:TPU:0, one launch (start us, length us, event | category | flops | bytes accessed | tf_op | source)
XLA Modules:
  0.0 180.2 jit_solution(17995431831905621239)
XLA Ops:
  0.6 81.2 %shard_map.77 = (f32[4,16,16,1024]{3,2,1,0:T(8,128)}, f32[16,256]{1,0:T(8,128)}, f32[32,1,512]{2,1,0:T(1,128)}) custom-call(f32[4,16,16,1024]{3,2,1,0:T(8,128)} %state_ref.1, f32[16,16,1024]{2,1,0:T(8,128)} %diff_ref.1, s32[1,32,512]{2,1,0:T(8,128)} %cells_ref.3, s32[16,256]{1,0:T(8,128)} %slots_ref.1, f32[16,256]{1,0:T(8,128)} %units_ref.1, f32[1,256]{1,0:T(1,128)} %bitcast.1), custom_call_target="tpu_custom_call" | custom-call | tf_op jit(solution)/shard_map/pallas_call | solution.py:264
  81.9 0.0 copy-start
  81.9 97.7 %shard_map.78 = f32[4,16,16,1024]{3,2,1,0:T(8,128)} custom-call(f32[32,1,512]{2,1,0:T(1,128)} %get-tuple-element.5.flow_ref, s32[1,32,512]{2,1,0:T(8,128)} %cells_ref.3, f32[4,16,16,1024]{3,2,1,0:T(8,128)} %get-tuple-element.6.fresh_ref.rest_ref, f32[4,16,16,1024]{3,2,1,0:T(8,128)} %get-tuple-element.6.fresh_ref.rest_ref), custom_call_target="tpu_custom_call" | custom-call | tf_op jit(solution)/shard_map/pallas_call | solution.py:350
  179.6 0.0 copy-done
  179.6 0.6 copy.9
Async XLA Ops:
  81.9 97.8 %copy-start = (f32[16,256]{1,0:T(8,128)S(1)}, f32[16,256]{1,0:T(8,128)}, u32[]{:S(2)}) copy-start(f32[16,256]{1,0:T(8,128)} %get-tuple-element.11) | copy-start | bytes 49156
